TPU v7x, 32 devices: a whole 2x2x4 slice. The times are simulated.
32 devices in a mesh: lat: 4 (over x, core), lon: 8 (over z, y).
Axes of the slice: x: 2, y: 2, z: 4, core: 2. Of those that a mesh axis runs over, the one named last changes fastest.
Arguments:
- fine_tokens: bfloat16 [2, 48, 96, 512], P(None, 'lat', 'lon'), may hold values from -6 to 6
- qkv_weight: bfloat16 [512, 1536], P(None, 'lat'), may hold values from -2 to 2
- proj_weight: bfloat16 [512, 512], P(None, 'lat'), may hold values from -0.25 to 0.25
- merge_one: bfloat16 [2048, 1024], P(None, 'lat'), may hold values from -0.125 to 0.125
- merge_two: bfloat16 [4096, 2048], P('lon'), may hold values from -0.09375 to 0.09375
- mlp_in: bfloat16 [2048, 8192], P(None, 'lon'), may hold values from -0.125 to 0.125
- mlp_out: bfloat16 [8192, 2048], P('lon'), may hold values from -0.125 to 0.125
- split_weight: bfloat16 [2048, 4096], P(None, 'lon'), may hold values from -0.125 to 0.125
Outputs:
- fine_out: float32 [2, 48, 96, 512], P(None, 'lat', 'lon')
- mid_out: float32 [2, 24, 48, 1024], P(None, 'lat', 'lon')
All inputs are finite; a program needn't handle non-finite values.
Results may differ from a plain program's by a relative error of at most 0.029.
Values may be sent and summed in bfloat16 or wider, within the bound.
A program may use at most 64 MiB of HBM per device.

v0:
```python
import functools
import math

import jax
import jax.numpy as jnp
from jax import lax
from jax.experimental import pallas as pl
from jax.experimental.pallas import tpu as pltpu
from jax.sharding import PartitionSpec as P

MID = 1024
HEADS = 8
WIN_R = 6
WIN_C = 12
SHIFT_R = 3
SHIFT_C = 6


def layer_norm(values):
    centre = jnp.mean(values, axis=-1, keepdims=True)
    shifted = values - centre
    spread = jnp.mean(shifted * shifted, axis=-1, keepdims=True)
    return shifted * lax.rsqrt(spread + 1e-05)


def cat_four(grid):
    lev, rows, cols, width = grid.shape
    grid = grid.reshape(lev, rows // 2, 2, cols // 2, 2, width).transpose(0, 1, 3, 2, 4, 5)
    return grid.reshape(lev * (rows // 2) * (cols // 2), 4 * width)


def coarse_kernel(
    blocks_ref, two_hbm, in_hbm, out_hbm, split_hbm, pieces_ref,
    two, w_in, w_out, split, landed, features, sent, summed, own, gathered, normed, act,
    sent2, summed2, gathered2, cols, sent3, landed3,
    load_sem, send_sem, recv_sem, relay_send, relay_recv,
):
    count = lax.axis_size("lon")
    me = lax.axis_index("lon")
    own_count = blocks_ref.shape[1]
    width = own.shape[1]
    loads = [
        pltpu.make_async_copy(source, target, load_sem.at[index])
        for index, (source, target) in enumerate(
            ((two_hbm, two), (in_hbm, w_in), (out_hbm, w_out), (split_hbm, split))
        )
    ]
    for load in loads:
        load.start()
    barrier = pltpu.get_barrier_semaphore()

    def greet(step, carry):
        peer = lax.rem(me + step, count)
        pl.semaphore_signal(
            barrier, inc=1, device_id={"lon": peer}, device_id_type=pl.DeviceIdType.MESH
        )
        return carry

    lax.fori_loop(1, count, greet, 0)
    pl.semaphore_wait(barrier, count - 1)

    def copy_to(phase, peer, source, target):
        return pltpu.make_async_remote_copy(
            src_ref=source,
            dst_ref=target.at[me],
            send_sem=send_sem.at[phase, peer],
            recv_sem=recv_sem.at[phase, me],
            device_id={"lon": peer},
            device_id_type=pl.DeviceIdType.MESH,
        )

    def wait_from(phase, target):
        def body(step, carry):
            peer = lax.rem(me + step, count)
            pltpu.make_async_remote_copy(
                src_ref=target.at[peer],
                dst_ref=target.at[peer],
                send_sem=send_sem.at[phase, peer],
                recv_sem=recv_sem.at[phase, peer],
                device_id={"lon": peer},
                device_id_type=pl.DeviceIdType.MESH,
            ).wait_recv()
            return carry

        lax.fori_loop(1, count, body, 0)

    def wait_sent(phase, source_of, target):
        def body(step, carry):
            peer = lax.rem(me + step, count)
            copy_to(phase, peer, source_of(peer), target).wait_send()
            return carry

        lax.fori_loop(1, count, body, 0)

    def scatter_products(phase, left, weight, send, target):
        def product(peer):
            cut = pl.ds(pl.multiple_of(peer * width, width), width)
            return jnp.dot(left[...], weight[:, cut], preferred_element_type=jnp.float32)

        def body(step, carry):
            peer = lax.rem(me + step, count)
            send[peer] = product(peer).astype(jnp.bfloat16)
            copy_to(phase, peer, send.at[peer], target).start()
            return carry

        lax.fori_loop(1, count, body, 0)
        total = product(me)
        wait_from(phase, target)

        def add(step, total):
            return total + target[lax.rem(me + step, count)].astype(jnp.float32)

        return lax.fori_loop(1, count, add, total)

    chips = count // 2
    z, y = me // 2, lax.rem(me, 2)
    partner = me + 1 - 2 * y
    up, down, over = 0, 1, 2

    def hop(source, target, sent_sem, came_sem, peer):
        return pltpu.make_async_remote_copy(
            src_ref=source,
            dst_ref=target,
            send_sem=sent_sem,
            recv_sem=came_sem,
            device_id={"lon": peer},
            device_id_type=pl.DeviceIdType.MESH,
        )

    def relay(phase, target, kind, block, peer):
        return hop(
            target.at[block],
            target.at[block],
            relay_send.at[phase, kind, block],
            relay_recv.at[phase, block],
            peer,
        )

    def relays(phase, target, act_on, arriving):
        pl.when(z < chips - 1)(lambda: act_on(relay(phase, target, up, me, me + 2)))
        pl.when(z > 0)(lambda: act_on(relay(phase, target, down, me, me - 2)))
        act_on(relay(phase, target, over, me, partner))
        for far in range(1, chips):

            @pl.when(z - far >= 0)
            def _():
                block = me - 2 * far
                if arriving:
                    relay(phase, target, up, block, me - 2).wait_recv()
                pl.when(z < chips - 1)(
                    lambda: act_on(relay(phase, target, up, block, me + 2))
                )
                act_on(relay(phase, target, over, block, partner))

            @pl.when(z + far < chips)
            def _():
                block = me + 2 * far
                if arriving:
                    relay(phase, target, down, block, me + 2).wait_recv()
                pl.when(z > 0)(lambda: act_on(relay(phase, target, down, block, me - 2)))
                act_on(relay(phase, target, over, block, partner))

    def gather(phase, target):
        relays(phase, target, lambda copy: copy.start(), True)
        for row in range(chips):
            relay(phase, target, over, 2 * row + 1 - y, partner).wait_recv()

    def wait_gather(phase, target):
        relays(phase, target, lambda copy: copy.wait_send(), False)

    def first(step, carry):
        peer = lax.rem(me + step, count)
        copy_to(0, peer, blocks_ref.at[peer], landed).start()
        return carry

    lax.fori_loop(1, count, first, 0)
    landed[me] = blocks_ref[me]
    wait_from(0, landed)
    for index in range(count):
        features[index * own_count : (index + 1) * own_count] = landed[index].astype(jnp.float32)
    normed[:, : features.shape[1]] = features[...].astype(jnp.bfloat16)
    loads[0].wait()
    merged = scatter_products(1, normed.at[:, : features.shape[1]], two, sent, summed)
    own[...] = merged
    gathered[me] = merged.astype(jnp.bfloat16)
    gather(0, gathered)

    total_width = count * width
    centre = gathered[0].astype(jnp.float32).sum(axis=-1, keepdims=True)
    for index in range(1, count):
        centre += gathered[index].astype(jnp.float32).sum(axis=-1, keepdims=True)
    centre = centre / total_width
    spread = jnp.zeros_like(centre)
    for index in range(count):
        shifted = gathered[index].astype(jnp.float32) - centre
        spread += (shifted * shifted).sum(axis=-1, keepdims=True)
    scale = lax.rsqrt(spread / total_width + 1e-05)
    for index in range(count):
        shifted = gathered[index].astype(jnp.float32) - centre
        normed[:, index * width : (index + 1) * width] = (shifted * scale).astype(jnp.bfloat16)
    loads[1].wait()

    tile = min(256, act.shape[1])

    def hidden(index, carry):
        cut = pl.ds(pl.multiple_of(index * tile, tile), tile)
        values = jnp.dot(normed[...], w_in[:, cut], preferred_element_type=jnp.float32)
        act[:, cut] = jax.nn.gelu(values).astype(jnp.bfloat16)
        return carry

    lax.fori_loop(0, act.shape[1] // tile, hidden, 0)
    loads[2].wait()
    mlp = scatter_products(3, act, w_out, sent2, summed2)
    gathered2[me] = (own[...] + mlp).astype(jnp.bfloat16)
    gather(1, gathered2)
    for index in range(count):
        normed[:, index * width : (index + 1) * width] = gathered2[index]
    loads[3].wait()
    cols[...] = jnp.dot(normed[...], split[...], preferred_element_type=jnp.float32)
    for index in range(count):
        sent3[index] = cols[index * own_count : (index + 1) * own_count].astype(jnp.bfloat16)

    def last(step, carry):
        peer = lax.rem(me + step, count)
        copy_to(5, peer, sent3.at[peer], landed3).start()
        return carry

    lax.fori_loop(1, count, last, 0)
    landed3[me] = sent3[me]
    wait_from(5, landed3)
    pieces_ref[...] = landed3[...]
    wait_sent(0, lambda peer: blocks_ref.at[peer], landed)
    wait_sent(1, lambda peer: sent.at[peer], summed)
    wait_gather(0, gathered)
    wait_sent(3, lambda peer: sent2.at[peer], summed2)
    wait_gather(1, gathered2)
    wait_sent(5, lambda peer: sent3.at[peer], landed3)


def coarse_in_one(blocks, merge_two, mlp_in, mlp_out, split_weight):
    count, own_count, depth = blocks.shape
    tokens, top = count * own_count, merge_two.shape[1]
    width, hidden, split_width = top // count, mlp_in.shape[1], split_weight.shape[1]
    low = jnp.bfloat16
    whole = pl.BlockSpec(memory_space=pltpu.VMEM)
    apart = pl.BlockSpec(memory_space=pl.ANY)
    return pl.pallas_call(
        coarse_kernel,
        out_shape=jax.ShapeDtypeStruct((count, own_count, split_width), low),
        in_specs=[whole, apart, apart, apart, apart],
        out_specs=whole,
        scratch_shapes=[
            pltpu.VMEM(merge_two.shape, low),
            pltpu.VMEM(mlp_in.shape, low),
            pltpu.VMEM(mlp_out.shape, low),
            pltpu.VMEM(split_weight.shape, low),
            pltpu.VMEM((count, own_count, depth), low),
            pltpu.VMEM((tokens, depth), jnp.float32),
            pltpu.VMEM((count, tokens, width), low),
            pltpu.VMEM((count, tokens, width), low),
            pltpu.VMEM((tokens, width), jnp.float32),
            pltpu.VMEM((count, tokens, width), low),
            pltpu.VMEM((tokens, top), low),
            pltpu.VMEM((tokens, hidden), low),
            pltpu.VMEM((count, tokens, width), low),
            pltpu.VMEM((count, tokens, width), low),
            pltpu.VMEM((count, tokens, width), low),
            pltpu.VMEM((tokens, split_width), jnp.float32),
            pltpu.VMEM((count, own_count, split_width), low),
            pltpu.VMEM((count, own_count, split_width), low),
            pltpu.SemaphoreType.DMA((4,)),
            pltpu.SemaphoreType.DMA((6, count)),
            pltpu.SemaphoreType.DMA((6, count)),
            pltpu.SemaphoreType.DMA((2, 3, count)),
            pltpu.SemaphoreType.DMA((2, count)),
        ],
        compiler_params=pltpu.CompilerParams(
            collective_id=0, has_side_effects=True, vmem_limit_bytes=60 * 1024 * 1024
        ),
    )(blocks, merge_two, mlp_in, mlp_out, split_weight)


def coarse_apart(normed2, merge_two, mlp_in, mlp_out, split_weight):
    own_count = normed2.shape[0]
    feature_parts = lax.all_to_all(normed2, "lon", split_axis=1, concat_axis=0, tiled=True)
    partial_value = jnp.dot(feature_parts, merge_two, preferred_element_type=jnp.float32)
    merged2 = lax.psum(partial_value.astype(jnp.bfloat16), "lon").astype(jnp.float32)
    normed3 = layer_norm(merged2).astype(jnp.bfloat16)
    act = jax.nn.gelu(jnp.dot(normed3, mlp_in, preferred_element_type=jnp.float32)).astype(
        jnp.bfloat16
    )
    mlp_own = lax.psum_scatter(
        jnp.dot(act, mlp_out, preferred_element_type=jnp.float32).astype(jnp.bfloat16),
        "lon",
        scatter_dimension=0,
        tiled=True,
    ).astype(jnp.float32)
    own_merged = lax.dynamic_slice_in_dim(merged2, lax.axis_index("lon") * own_count, own_count, 0)
    coarse = (own_merged + mlp_own).astype(jnp.bfloat16)
    split_cols = jnp.dot(
        lax.all_gather(coarse, "lon", axis=0, tiled=True),
        split_weight,
        preferred_element_type=jnp.float32,
    ).astype(jnp.bfloat16)
    return lax.all_to_all(split_cols, "lon", split_axis=0, concat_axis=1, tiled=True)


def halo_kernel(direction, shards, *refs):
    edges, weights = refs[:3], refs[3 : 3 + shards]
    came, wholes = refs[3 + shards : 6 + shards], refs[6 + shards : 6 + 2 * shards]
    edge_send, edge_recv, own_sem, weight_send, weight_recv = refs[6 + 2 * shards :]
    lat_count, lon_count = lax.axis_size("lat"), lax.axis_size("lon")
    row, col = lax.axis_index("lat"), lax.axis_index("lon")
    mesh = pl.DeviceIdType.MESH

    def beside(sign):
        next_row = lax.rem(row + sign + lat_count, lat_count)
        next_col = lax.rem(col + sign + lon_count, lon_count)
        return (next_row, col), (row, next_col), (next_row, next_col)

    other_core = row + 1 - 2 * lax.rem(row, 2)
    other_chip = lax.rem(row + 2, 4)
    side = lax.rem(col, 2)
    pair = col + 1 - 2 * side
    partners = beside(1) + beside(-1)
    if shards:
        partners += ((other_core, col), (other_chip, col), (row, pair))
    barrier = pltpu.get_barrier_semaphore()
    for partner in partners:
        pl.semaphore_signal(barrier, inc=1, device_id=partner, device_id_type=mesh)
    pl.semaphore_wait(barrier, len(partners))

    copies = []
    for index, target in enumerate(beside(direction)):
        copies.append(
            pltpu.make_async_remote_copy(
                src_ref=edges[index],
                dst_ref=came[index],
                send_sem=edge_send.at[index],
                recv_sem=edge_recv.at[index],
                device_id=target,
                device_id_type=mesh,
            )
        )
    for copy in copies:
        copy.start()

    def columns(index, owner):
        width = weights[index].shape[1]
        return wholes[index].at[:, pl.ds(pl.multiple_of(owner * width, width), width)]

    def half(ref, index, which):
        depth = weights[index].shape[0] // 2
        return ref.at[pl.ds(pl.multiple_of(which * depth, depth), depth)]

    def send(index, kind, source, target, device):
        copy = pltpu.make_async_remote_copy(
            src_ref=source,
            dst_ref=target,
            send_sem=weight_send.at[index, kind],
            recv_sem=weight_recv.at[index, kind],
            device_id=device,
            device_id_type=mesh,
        )
        copy.start()
        return copy

    moves = []
    for index in range(shards):
        mine, held = weights[index], columns(index, row)
        away = send(
            index, 0, half(mine, index, side), half(held, index, side), (other_chip, col)
        )
        moves.append([away, send(index, 1, mine, held, (other_core, col))])
        pltpu.make_async_copy(mine, held, own_sem.at[index]).start()
    for index in range(shards):
        moves[index][0].wait_recv()
        part = half(columns(index, other_chip), index, side)
        moves[index].append(send(index, 2, part, part, (row, pair)))
        moves[index].append(send(index, 3, part, part, (other_core, col)))
    for index in range(shards):
        moves[index][2].wait_recv()
        part = half(columns(index, other_chip), index, 1 - side)
        moves[index].append(send(index, 4, part, part, (other_core, col)))
    for index in range(shards):
        away, core, paired, first, second = moves[index]
        for copy in (away, core, paired, first, second):
            copy.wait_send()
        for copy in (core, first, second):
            copy.wait_recv()
        pltpu.make_async_copy(weights[index], columns(index, row), own_sem.at[index]).wait()
    for copy in copies:
        copy.wait()


def exchange(edges, direction, weights, identity):
    whole = pl.BlockSpec(memory_space=pltpu.VMEM)
    shards = len(weights)
    outs = [jax.ShapeDtypeStruct(edge.shape, edge.dtype) for edge in edges]
    outs += [
        jax.ShapeDtypeStruct((part.shape[0], 4 * part.shape[1]), part.dtype) for part in weights
    ]
    return pl.pallas_call(
        functools.partial(halo_kernel, direction, shards),
        out_shape=outs,
        in_specs=[whole] * (3 + shards),
        out_specs=[whole] * (3 + shards),
        scratch_shapes=[
            pltpu.SemaphoreType.DMA((3,)),
            pltpu.SemaphoreType.DMA((3,)),
            pltpu.SemaphoreType.DMA((max(shards, 1),)),
            pltpu.SemaphoreType.DMA((max(shards, 1), 5)),
            pltpu.SemaphoreType.DMA((max(shards, 1), 5)),
        ],
        compiler_params=pltpu.CompilerParams(collective_id=identity, has_side_effects=True),
    )(*edges, *weights)


def lat_swap(value, mask):
    return lax.ppermute(value, "lat", [(index, index ^ mask) for index in range(4)])


def in_owner_order(parts):
    index = lax.axis_index("lat")
    odd, high = index % 2 == 1, index >= 2
    a, b, c, d = parts
    a, b = jnp.where(odd, b, a), jnp.where(odd, a, b)
    c, d = jnp.where(odd, d, c), jnp.where(odd, c, d)
    a, c = jnp.where(high, c, a), jnp.where(high, a, c)
    b, d = jnp.where(high, d, b), jnp.where(high, b, d)
    return jnp.concatenate((a, b, c, d), axis=-1)


def on_device(
    fine_tokens, qkv_weight, proj_weight, merge_one, merge_two, mlp_in, mlp_out, split_weight
):
    levels, rows, cols, width = fine_tokens.shape
    lat_count = lax.axis_size("lat")
    head_dim = width // HEADS
    edges = (
        fine_tokens[:, :SHIFT_R, SHIFT_C:],
        fine_tokens[:, SHIFT_R:, :SHIFT_C],
        fine_tokens[:, :SHIFT_R, :SHIFT_C],
    )
    if lat_count == 4 and lax.axis_size("lon") % 2 == 0:
        row_came, col_came, both_came, full_qkv, full_proj = exchange(
            edges, -1, (qkv_weight, proj_weight), 1
        )
        merge_one, row_came = lax.optimization_barrier((merge_one, row_came))
        merge_far = lat_swap(merge_one, 2)
        merge_parts = (merge_one, lat_swap(merge_one, 1), merge_far, lat_swap(merge_far, 1))
    else:
        row_came, col_came, both_came = exchange(edges, -1, (), 1)
        full_qkv = lax.all_gather(qkv_weight, "lat", axis=1, tiled=True)
        full_proj = lax.all_gather(proj_weight, "lat", axis=1, tiled=True)
    upper = jnp.concatenate([fine_tokens[:, SHIFT_R:, SHIFT_C:], col_came], axis=2)
    lower = jnp.concatenate([row_came, both_came], axis=2)
    moved = jnp.concatenate([upper, lower], axis=1)
    normed = layer_norm(moved.astype(jnp.float32)).astype(jnp.bfloat16).reshape(-1, width)
    qkv = jnp.dot(normed, full_qkv, preferred_element_type=jnp.float32).astype(jnp.bfloat16)
    row_wins = rows // WIN_R
    col_wins = cols // WIN_C
    wins = row_wins * col_wins
    tokens = levels * WIN_R * WIN_C
    parts = qkv.reshape(levels, row_wins, WIN_R, col_wins, WIN_C, 3, HEADS, head_dim)
    parts = parts.transpose(1, 3, 0, 2, 4, 5, 6, 7).reshape(wins, tokens, 3, HEADS, head_dim)
    scores = jnp.einsum(
        "wqhd,wkhd->whqk", parts[:, :, 0], parts[:, :, 1], preferred_element_type=jnp.float32
    )
    scores = scores / math.sqrt(head_dim)
    global_rows = lax.axis_index("lat") * rows + jnp.arange(rows, dtype=jnp.int32)
    wrapped = (global_rows >= rows * lat_count - SHIFT_R).astype(jnp.int32).reshape(row_wins, WIN_R)
    labels = jnp.broadcast_to(
        wrapped[:, None, None, :, None], (row_wins, col_wins, levels, WIN_R, WIN_C)
    )
    labels = labels.reshape(wins, tokens)
    allowed = labels[:, :, None] == labels[:, None, :]
    scores = jnp.where(allowed[:, None], scores, jnp.float32(-1000000000.0))
    top = jnp.max(scores, axis=-1, keepdims=True)
    expo = jnp.exp(scores - top)
    probs = (expo / jnp.sum(expo, axis=-1, keepdims=True)).astype(jnp.bfloat16)
    heads_out = jnp.einsum(
        "whqk,wkhd->wqhd", probs, parts[:, :, 2], preferred_element_type=jnp.float32
    )
    heads_out = heads_out.astype(jnp.bfloat16).reshape(
        row_wins, col_wins, levels, WIN_R, WIN_C, width
    )
    heads_out = heads_out.transpose(2, 0, 3, 1, 4, 5).reshape(-1, width)
    attn = jnp.dot(heads_out, full_proj, preferred_element_type=jnp.float32).astype(jnp.bfloat16)
    attn = attn.reshape(levels, rows, cols, width)
    edges = (
        attn[:, rows - SHIFT_R :, : cols - SHIFT_C],
        attn[:, : rows - SHIFT_R, cols - SHIFT_C :],
        attn[:, rows - SHIFT_R :, cols - SHIFT_C :],
    )
    row_came, col_came, both_came = exchange(edges, 1, (), 2)
    upper = jnp.concatenate([both_came, row_came], axis=2)
    lower = jnp.concatenate([col_came, attn[:, : rows - SHIFT_R, : cols - SHIFT_C]], axis=2)
    back = jnp.concatenate([upper, lower], axis=1)
    fine_out = fine_tokens.astype(jnp.float32) + back.astype(jnp.float32)
    normed1 = layer_norm(cat_four(fine_out)).astype(jnp.bfloat16)
    if lat_count == 4 and lax.axis_size("lon") % 2 == 0:
        merged1 = in_owner_order(
            [
                jnp.dot(normed1, part, preferred_element_type=jnp.float32).astype(jnp.bfloat16)
                for part in merge_parts
            ]
        )
    else:
        merge_all = lax.all_gather(merge_one, "lat", axis=1, tiled=True)
        merged1 = jnp.dot(normed1, merge_all, preferred_element_type=jnp.float32)
        merged1 = merged1.astype(jnp.bfloat16)
    merged1 = merged1.reshape(levels, rows // 2, cols // 2, MID)
    normed2 = layer_norm(cat_four(merged1.astype(jnp.float32))).astype(jnp.bfloat16)
    count = lax.axis_size("lon")
    if count % 2 == 0 and merge_two.shape[1] % (count * 128) == 0:
        blocks = normed2.reshape(normed2.shape[0], count, -1).transpose(1, 0, 2)
        pieces = coarse_in_one(blocks, merge_two, mlp_in, mlp_out, split_weight)
        pieces = pieces.transpose(1, 0, 2)
    else:
        pieces = coarse_apart(normed2, merge_two, mlp_in, mlp_out, split_weight)
    pieces = pieces.reshape(levels, rows // 4, cols // 4, 2, 2, MID).transpose(0, 1, 3, 2, 4, 5)
    pieces = pieces.reshape(levels, rows // 2, cols // 2, MID)
    mid_out = merged1.astype(jnp.float32) + pieces.astype(jnp.float32)
    return (fine_out, mid_out)


def solution(mesh):
    return jax.shard_map(
        on_device,
        mesh=mesh,
        in_specs=(
            P(None, "lat", "lon", None),
            P(None, "lat"),
            P(None, "lat"),
            P(None, "lat"),
            P("lon", None),
            P(None, "lon"),
            P("lon", None),
            P(None, "lon"),
        ),
        out_specs=(P(None, "lat", "lon", None), P(None, "lat", "lon", None)),
        check_vma=False,
    )
```

profile of v0, /device:TPU:0, one launch (start us, length us, event | category | flops | bytes accessed | tf_op | source)
XLA Modules:
  0.0 140.1 jit_solution(17087167868390770992)
XLA Ops:
  0.6 1.1 fusion.34
  1.7 0.8 fusion.35
  2.6 0.7 copy.128.refs_1_
  3.3 0.6 copy.127.refs_0_
  3.9 0.6 copy.129.refs_2_
  4.5 21.6 %shard_map.95 = (bf16[2,3,6,512]{3,2,1,0:T(8,128)(2,1)}, bf16[2,9,6,512]{3,2,1,0:T(8,128)(2,1)}, bf16[2,3,6,512]{3,2,1,0:T(8,128)(2,1)}, bf16[512,1536]{1,0:T(8,128)(2,1)}, bf16[512,512]{1,0:T(8,128)(2,1)}) custom-call(bf16[2,3,6,512]{3,2,1,0:T(8,128)(2,1)} %copy.127.refs_0_, bf16[2,9,6,512]{3,2,1,0:T(8,128)(2,1)} %copy.128.refs_1_, ...), custom_call_target="tpu_custom_call" | custom-call | tf_op jit(solution)/shard_map/pallas_call | solution.py:403
  26.2 0.1 collective-permute-start.2
  26.2 1.7 %collective-permute-start = (bf16[2048,256]{1,0:T(8,128)(2,1)}, bf16[2048,256]{1,0:T(8,128)(2,1)}, u32[]{:S(2)}, u32[]{:S(2)}) collective-permute-start(bf16[2048,256]{1,0:T(8,128)(2,1)} %param.11), channel_id=1, source_target_pairs={{0,16},{8,24},{16,0},{24,8},{1,17},{9,25},{17,1},{25,9},{2,18},{10... | collective-permute-start | bytes 3145736 | tf_op jit(solution)/shard_map/ppermute | solution.py:420
  27.9 1.2 fusion.30
  29.1 1.3 multiply_reduce_fusion
  30.4 0.1 div.39
  30.5 1.1 maximum_convert_fusion
  31.6 0.1 rsqrt.34
  31.7 0.1 reshape.175
  31.8 2.1 %convolution_convert_fusion = bf16[288,1536]{1,0:T(8,128)(2,1)S(1)} fusion(bf16[512,1536]{1,0:T(8,128)(2,1)} %get-tuple-element.16, f32[288,512]{1,0:T(8,128)S(1)} %reshape.175, f32[288]{0:T(512)S(1)} %rsqrt.34, f32[288]{0:T(512)S(1)} %div.39), kind=kOutput, calls=%fused_computation.1 | convolution fusion | flops 453869568 | bytes 3049728 | tf_op jit(solution)/shard_map/dot_general | solution.py:460
  33.9 1.1 reshape.167
  35.0 0.3 copy.90
  35.3 0.3 fusion.31
  35.6 0.4 copy.111
  36.0 0.4 copy.112
  36.4 0.1 broadcast_in_dim.16
  36.5 0.1 broadcast_in_dim.17
  36.6 0.1 broadcast_compare_fusion
  36.7 0.4 copy.110
  37.1 2.4 %fusion.36 = (f32[2,8,144]{2,1,0:T(8,128)S(1)}, f32[2,8,144,144]{2,3,1,0:T(8,128)}) fusion(pred[2,144,144]{1,2,0:T(8,128)(4,1)S(1)} %broadcast_compare_fusion, bf16[2,144,1,8,64]{1,4,3,0,2:T(8,128)(2,1)S(1)} %copy.112, bf16[2,144,1,8,64]{1,4,3,0,2:T(8,128)(2,1)S(1)} %copy.111), kind=kOutput, calls=%fused_computation.62 | convolution fusion | flops 43794576 | bytes 1967616 | tf_op jit(solution)/shard_map/sub | solution.py:480
  39.5 2.0 %fusion.2 = bf16[2,144,8,64]{1,3,2,0:T(8,128)(2,1)S(1)} fusion(f32[2,8,144,144]{2,3,1,0:T(8,128)} %get-tuple-element.48, f32[2,8,144]{2,1,0:T(8,128)S(1)} %get-tuple-element.47, bf16[2,144,1,8,64]{1,4,3,0,2:T(8,128)(2,1)S(1)} %copy.110), kind=kOutput, calls=%fused_computation.7 | convolution fusion | flops 43278336 | bytes 1926144 | tf_op jit(solution)/shard_map/whqk,wkhd->wqhd/dot_general | solution.py:482
  41.5 0.5 copy.95
  42.1 0.3 reshape.169
  42.4 0.1 reshape.170
  42.6 0.3 convolution_convert_fusion.2
  42.9 0.1 reshape.171
  43.0 0.7 fusion.33
  43.7 0.6 fusion.32
  44.3 12.4 %shard_map.96 = (bf16[2,3,6,512]{3,2,1,0:T(8,128)(2,1)}, bf16[2,9,6,512]{3,2,1,0:T(8,128)(2,1)}, bf16[2,3,6,512]{3,2,1,0:T(8,128)(2,1)}) custom-call(bf16[2,3,6,512]{3,2,1,0:T(8,128)(2,1)} %get-tuple-element.36.refs_0_, bf16[2,9,6,512]{3,2,1,0:T(8,128)(2,1)} %get-tuple-element.37.refs_1_, bf16[2,3,6,512]{3,2,1,0:T(8,128)(2,1)} %get-tuple-element.35.refs_2_), custom_call_target="tpu_custom_call" | custom-call | tf_op jit(solution)/shard_map/pallas_call | solution.py:403
  56.7 1.1 convert_add_fusion
  57.8 0.5 copy.107
  58.3 0.2 reduce_sum.66
  58.6 0.5 multiply_reduce_fusion.1
  59.0 0.3 copy.98
  59.3 0.1 copy.99
  59.5 0.1 copy.100
  59.6 0.1 rsqrt.36
  59.7 0.5 reshape.173
  60.2 0.1 div.46
  60.3 0.1 collective-permute-start.1
  60.4 0.1 multiply_convert_fusion
  60.5 0.3 convolution_convert_fusion.3
  60.8 1.5 %convolution_convert_fusion.5 = bf16[72,256]{1,0:T(8,128)(2,1)S(1)} fusion(bf16[72,2048]{1,0:T(8,128)(2,1)S(1)} %multiply_convert_fusion, bf16[2048,256]{1,0:T(8,128)(2,1)} %collective-permute-done), kind=kOutput, calls=%fused_computation.14 | convolution fusion | flops 75515904 | bytes 1380352 | tf_op jit(solution)/shard_map/dot_general | solution.py:505
  62.4 1.5 %convolution_convert_fusion.4 = bf16[72,256]{1,0:T(8,128)(2,1)S(1)} fusion(bf16[72,2048]{1,0:T(8,128)(2,1)S(1)} %multiply_convert_fusion, bf16[2048,256]{1,0:T(8,128)(2,1)} %collective-permute-done.2), kind=kOutput, calls=%fused_computation.13 | convolution fusion | flops 75515904 | bytes 1380352 | tf_op jit(solution)/shard_map/dot_general | solution.py:505
  63.9 0.3 broadcast_select_fusion.7
  64.3 0.2 reshape.178
  64.5 0.2 fusion.29
  64.7 0.3 multiply_reduce_fusion.2
  65.0 0.1 div.49
  65.1 0.1 rsqrt.38
  65.2 0.2 reshape.174
  65.5 0.9 fusion.14.blocks_ref
  66.3 71.1 %shard_map.97 = bf16[8,18,512]{2,1,0:T(8,128)(2,1)} custom-call(bf16[8,18,512]{2,1,0:T(8,128)(2,1)} %fusion.14.blocks_ref, bf16[512,2048]{1,0:T(8,128)(2,1)} %two_hbm.1, bf16[2048,1024]{1,0:T(8,128)(2,1)} %in_hbm.1, bf16[1024,2048]{1,0:T(8,128)(2,1)} %out_hbm.1, bf16[2048,512]{1,0:T(8,128)(2,1)} %split_hbm.1), custom_call_target="tpu_custom_call" | custom-call | tf_op jit(solution)/shard_map/pallas_call | solution.py:247
  137.4 1.0 convert_bitcast_fusion
  138.4 0.2 copy.104
  138.6 0.2 reshape.179
  138.8 0.2 copy.105
  139.0 0.1 copy_add_fusion
  139.2 0.9 copy.108
  (23 shorter events, 0.3 us)
Async XLA Ops:
  26.2 36.2 %collective-permute-start.2 = (bf16[2048,256]{1,0:T(8,128)(2,1)}, bf16[2048,256]{1,0:T(8,128)(2,1)}, u32[]{:S(2)}, u32[]{:S(2)}) collective-permute-start(bf16[2048,256]{1,0:T(8,128)(2,1)} %param.11), channel_id=1, source_target_pairs={{0,8},{8,0},{16,24},{24,16},{1,9},{9,1},{17,25},{25,17},{2,10},{10... | collective-permute-start | bytes 3145736 | tf_op jit(solution)/shard_map/ppermute | solution.py:420
  26.2 34.1 %collective-permute-start = (bf16[2048,256]{1,0:T(8,128)(2,1)}, bf16[2048,256]{1,0:T(8,128)(2,1)}, u32[]{:S(2)}, u32[]{:S(2)}) collective-permute-start(bf16[2048,256]{1,0:T(8,128)(2,1)} %param.11), channel_id=1, source_target_pairs={{0,16},{8,24},{16,0},{24,8},{1,17},{9,25},{17,1},{25,9},{2,18},{10... | collective-permute-start | bytes 3145736 | tf_op jit(solution)/shard_map/ppermute | solution.py:420
  41.5 1.0 copy-start.3
  42.1 14.7 %copy-start.1 = (bf16[2,12,12,512]{3,0,2,1:T(2,128)(2,1)S(1)}, bf16[2,12,12,512]{3,0,2,1:T(2,128)(2,1)}, u32[]{:S(2)}) copy-start(bf16[2,12,12,512]{3,0,2,1:T(2,128)(2,1)} %param.8) | copy-start | bytes 884740
  58.3 2.5 %copy-start = (f32[2,12,12,512]{3,0,2,1:T(2,128)}, f32[2,12,12,512]{3,0,2,1:T(2,128)S(1)}, u32[]{:S(2)}) copy-start(f32[2,12,12,512]{3,0,2,1:T(2,128)S(1)} %copy.107) | copy-start | bytes 1769476
  58.3 2.2 %copy-start.2 = (bf16[2048,256]{1,0:T(8,128)(2,1)S(1)}, bf16[2048,256]{1,0:T(8,128)(2,1)}, u32[]{:S(2)}) copy-start(bf16[2048,256]{1,0:T(8,128)(2,1)} %param.11) | copy-start | bytes 3145732
  60.3 3.6 %collective-permute-start.1 = (bf16[2048,256]{1,0:T(8,128)(2,1)}, bf16[2048,256]{1,0:T(8,128)(2,1)S(1)}, u32[]{:S(2)}, u32[]{:S(2)}) collective-permute-start(bf16[2048,256]{1,0:T(8,128)(2,1)} %collective-permute-done), channel_id=1, source_target_pairs={{0,8},{8,0},{16,24},{24,16},{1,9},{9,1},{17,25},{25,17},{2,10},{10... | collective-permute-start | bytes 3145736 | tf_op jit(solution)/shard_map/ppermute | solution.py:420
where the time goes:
time: 143 us; the launch traced here: 140 us
  Pallas kernels  105 us (73%)
  local copies, waits for them, and re-layouts  13.5 us (9%)
  matrix products  10.5 us (7%)
  other arithmetic  8.07 us (6%)
  starting transfers between devices  1.82 us (1%)
    pallas_call x1, Pallas kernels, coarse_in_one(): pl.pallas_call(coarse_kernel, out_shape=jax.ShapeDtypeStruct((count, own_...  71.1 us
    pallas_call x2, Pallas kernels, exchange(): pl.pallas_call(functools.partial(halo_kernel, direction, shards), out_sha...  34 us
    unnamed x17, local copies, waits for them, and re-layouts  4.59 us
    dot_general x4, matrix products, on_device(): jnp.dot(normed1, part, preferred_element_type=jnp.float32)  3.68 us
  transfers between devices with their start and end apart: 3, of which 0 were waited for; matrix products, arithmetic and copies ran while one was open for 17% of the time, Pallas kernels for 9%

commit v1 on v0

--- a/solution.py
+++ b/solution.py
@@ -431,7 +431,367 @@
     return jnp.concatenate((a, b, c, d), axis=-1)
 
 
-def on_device(
+def attend_kernel(
+    tok, qkv_hbm, proj_hbm, merge_hbm, fine_ref, merged_ref, blocks_ref,
+    wq, wp, wm, low, came_row, came_low, packed, normed, qkv, bias, heads, low_back, row_back,
+    attn, back_row, back_low, split_fine, cat, cat_low, parts, split_mid, cat2,
+    halo_send, halo_recv, own_sem, weight_send, weight_recv,
+):
+    lat_count, lon_count = lax.axis_size("lat"), lax.axis_size("lon")
+    row, col = lax.axis_index("lat"), lax.axis_index("lon")
+    mesh = pl.DeviceIdType.MESH
+    f32, low_type = jnp.float32, jnp.bfloat16
+    rows, slots, width = tok.shape
+    levels = 2
+    near = levels * SHIFT_C
+    edge = low.shape[1]
+    head_dim = width // HEADS
+
+    def beside(sign):
+        next_row = lax.rem(row + sign + lat_count, lat_count)
+        next_col = lax.rem(col + sign + lon_count, lon_count)
+        return (next_row, col), (row, next_col), (next_row, next_col)
+
+    other_core = row + 1 - 2 * lax.rem(row, 2)
+    other_chip = lax.rem(row + 2, 4)
+    far = lax.rem(other_core + 2, 4)
+    side = lax.rem(col, 2)
+    pair = col + 1 - 2 * side
+    low[...] = tok[...].astype(f32)[:, :edge].astype(low_type)
+    cat[...] = jnp.zeros_like(cat)
+    partners = beside(1) + beside(-1) + ((other_core, col), (other_chip, col), (row, pair))
+    barrier = pltpu.get_barrier_semaphore()
+    for partner in partners:
+        pl.semaphore_signal(barrier, inc=1, device_id=partner, device_id_type=mesh)
+    pl.semaphore_wait(barrier, len(partners))
+
+    shards = (qkv_hbm, proj_hbm, merge_hbm)
+    counts = WEIGHT_PIECES
+
+    def whole(index, owner):
+        if index == 1:
+            cut = proj_hbm.shape[1]
+            return wp.at[:, pl.ds(pl.multiple_of(owner * cut, cut), cut)]
+        return (wq if index == 0 else wm).at[owner]
+
+    def piece(ref, index, which, number):
+        depth = shards[index].shape[0] // 2
+        size = depth // counts[index]
+        start = pl.multiple_of(which * depth + number * size, size)
+        return ref.at[pl.ds(start, size)]
+
+    def send(index, kind, number, source, target, device):
+        place = kind * max(counts) + number
+        copy = pltpu.make_async_remote_copy(
+            src_ref=source,
+            dst_ref=target,
+            send_sem=weight_send.at[index, place],
+            recv_sem=weight_recv.at[index, place],
+            device_id=device,
+            device_id_type=mesh,
+        )
+        copy.start()
+        return copy
+
+    over, across, own = {}, {}, {}
+    first, second, third = {}, {}, {}
+
+    def send_over(index):
+        for number in range(counts[index]):
+            over[index, number] = send(
+                index, 0, number,
+                piece(shards[index], index, side, number),
+                piece(whole(index, row), index, side, number),
+                (other_chip, col),
+            )
+
+    def send_across(index):
+        across[index] = send(
+            index, 1, 0, shards[index], whole(index, row), (other_core, col)
+        )
+        own[index] = pltpu.make_async_copy(shards[index], whole(index, row), own_sem.at[index])
+        own[index].start()
+
+    def pass_on(index, number):
+        over[index, number].wait_recv()
+        held = piece(whole(index, other_chip), index, side, number)
+        first[index, number] = send(index, 2, number, held, held, (row, pair))
+        second[index, number] = send(index, 3, number, held, held, (other_core, col))
+
+    def pass_last(index, number):
+        first[index, number].wait_recv()
+        held = piece(whole(index, other_chip), index, 1 - side, number)
+        third[index, number] = send(index, 4, number, held, held, (other_core, col))
+
+    def wait_far(index):
+        for number in range(counts[index]):
+            second[index, number].wait_recv()
+            third[index, number].wait_recv()
+
+    def halo(place, source, target, device):
+        copy = pltpu.make_async_remote_copy(
+            src_ref=source,
+            dst_ref=target,
+            send_sem=halo_send.at[place],
+            recv_sem=halo_recv.at[place],
+            device_id=device,
+            device_id_type=mesh,
+        )
+        copy.start()
+        return copy
+
+    before, after = beside(-1), beside(1)
+    there = [
+        halo(0, low.at[SHIFT_R:], came_low.at[SHIFT_R:], before[1]),
+        halo(1, low.at[:SHIFT_R], came_low.at[:SHIFT_R], before[2]),
+    ]
+    send_over(0)
+    there.append(halo(2, tok.at[:SHIFT_R], came_row, before[0]))
+    send_across(0)
+    send_over(1)
+    send_across(1)
+    send_over(2)
+    send_across(2)
+
+    slot = lax.broadcasted_iota(jnp.int32, (1, edge, width), 1)
+    tokens = WIN_R * slots
+    wins = rows // WIN_R
+    key_row = lax.broadcasted_iota(jnp.int32, (tokens, tokens), 1) >= (WIN_R - SHIFT_R) * slots
+    query_row = lax.broadcasted_iota(jnp.int32, (tokens, tokens), 0) >= (WIN_R - SHIFT_R) * slots
+    last = jnp.where(row == lat_count - 1, f32(-1000000000.0), f32(0.0))
+    bias[...] = jnp.where(key_row == query_row, f32(0.0), last)
+
+    for number in range(counts[0]):
+        pass_on(0, number)
+    for copy in there:
+        copy.wait_recv()
+    packed[: rows - SHIFT_R] = tok[SHIFT_R:].astype(f32)
+    packed[rows - SHIFT_R :] = came_row[...].astype(f32)
+    packed[: rows - SHIFT_R, :edge] = jnp.where(
+        slot < near, came_low[SHIFT_R:].astype(f32), packed[: rows - SHIFT_R, :edge]
+    )
+    packed[rows - SHIFT_R :, :edge] = jnp.where(
+        slot < near, came_low[:SHIFT_R].astype(f32), packed[rows - SHIFT_R :, :edge]
+    )
+    for win in range(wins):
+        values = packed[win * WIN_R : (win + 1) * WIN_R].reshape(tokens, width)
+        normed[win * tokens : (win + 1) * tokens] = layer_norm(values).astype(low_type)
+
+    cut = qkv_hbm.shape[1]
+
+    def project(owner):
+        place = pl.ds(pl.multiple_of(owner * cut, cut), cut)
+        qkv[:, place] = jnp.dot(
+            normed[...], wq[owner], preferred_element_type=f32
+        ).astype(low_type)
+
+    own[0].wait()
+    project(row)
+    across[0].wait_recv()
+    project(other_core)
+    for number in range(counts[0]):
+        pass_last(0, number)
+    project(other_chip)
+    wait_far(0)
+    project(far)
+
+    for number in range(counts[1]):
+        pass_on(1, number)
+    pass_on(2, 0)
+
+    lane = lax.broadcasted_iota(jnp.int32, (1, 2 * head_dim), 1)
+    near_head = jnp.where(lane < head_dim, 1.0, 0.0).astype(low_type)
+    scale = 1.0 / math.sqrt(head_dim)
+
+    def attend(win):
+        place = pl.ds(win * tokens, tokens)
+
+        def head_pair(index, carry):
+            def columns(kind):
+                start = pl.multiple_of(kind * width + index * 2 * head_dim, 2 * head_dim)
+                return qkv[place, pl.ds(start, 2 * head_dim)]
+
+            query, key, value = columns(0), columns(1), columns(2)
+            outs = []
+            for mask in (near_head, 1 - near_head):
+                scores = lax.dot_general(
+                    query, key * mask, (((1,), (1,)), ((), ())), preferred_element_type=f32
+                )
+                scores = scores * scale
+                if win == wins - 1:
+                    scores = scores + bias[...]
+                expo = jnp.exp(scores - jnp.max(scores, axis=-1, keepdims=True))
+                total = jnp.sum(expo, axis=-1, keepdims=True)
+                out = jnp.dot(expo.astype(low_type), value, preferred_element_type=f32)
+                outs.append(out / total)
+            start = pl.multiple_of(index * 2 * head_dim, 2 * head_dim)
+            heads[place, pl.ds(start, 2 * head_dim)] = jnp.where(
+                lane < head_dim, outs[0], outs[1]
+            ).astype(low_type)
+            return carry
+
+        lax.fori_loop(0, HEADS // 2, head_pair, 0)
+
+    for win in range(wins):
+        attend(win)
+        if win == 0:
+            for number in range(counts[1]):
+                pass_last(1, number)
+        pass_on(2, win + 1)
+        pass_last(2, win)
+
+    own[1].wait()
+    across[1].wait_recv()
+    wait_far(1)
+    for win in range(wins):
+        values = jnp.dot(
+            heads[win * tokens : (win + 1) * tokens], wp[...], preferred_element_type=f32
+        )
+        values = values.astype(low_type).astype(f32).reshape(WIN_R, slots, width)
+        attn[win * WIN_R : (win + 1) * WIN_R] = values
+    low_back[...] = attn[:, :edge].astype(low_type)
+    row_back[...] = attn[rows - SHIFT_R :].astype(low_type)
+    kept = rows - SHIFT_R
+    back = [
+        halo(3, low_back.at[:kept], back_low.at[SHIFT_R:], after[1]),
+        halo(4, low_back.at[kept:], back_low.at[:SHIFT_R], after[2]),
+        halo(5, row_back, back_row, after[0]),
+    ]
+    for number in range(wins + 1, counts[2]):
+        pass_on(2, number)
+    for copy in back:
+        copy.wait_recv()
+
+    fine_ref[SHIFT_R:] = tok[SHIFT_R:].astype(f32) + attn[:kept]
+    fine_ref[:SHIFT_R] = tok[:SHIFT_R].astype(f32) + back_row[...].astype(f32)
+    fine_ref[:, :edge] = jnp.where(
+        slot < near,
+        tok[...].astype(f32)[:, :edge] + back_low[...].astype(f32),
+        fine_ref[:, :edge],
+    )
+
+    group = cat.shape[0] // rows
+    half_cols = slots // levels // 2
+    lanes = 128
+    for tile in range(width // lanes):
+        split_fine[tile] = fine_ref[:, :, tile * lanes : (tile + 1) * lanes]
+    for line in range(rows // 2):
+        for level in range(levels):
+            for part in range(4):
+                start = levels * (part % 2) + level
+                base = (line * levels + level) * group
+                for tile in range(width // lanes):
+                    place = part * width + tile * lanes
+                    cat[base : base + half_cols, place : place + lanes] = split_fine[
+                        tile, 2 * line + part // 2, pl.ds(start, half_cols, stride=2 * levels), :
+                    ]
+    for number in range(wins, counts[2]):
+        pass_last(2, number)
+    cat_low[...] = layer_norm(cat[...]).astype(low_type)
+    wide = merge_hbm.shape[1]
+
+    def merge(owner):
+        values = jnp.dot(cat_low[...], wm[owner], preferred_element_type=f32)
+        place = pl.ds(pl.multiple_of(owner * wide, wide), wide)
+        parts[:, place] = values.astype(low_type).astype(f32)
+
+    own[2].wait()
+    merge(row)
+    across[2].wait_recv()
+    merge(other_core)
+    merge(other_chip)
+    wait_far(2)
+    merge(far)
+    merged_ref[...] = parts[...].astype(low_type)
+    mid = parts.shape[1]
+    for tile in range(mid // lanes):
+        split_mid[tile] = parts[:, tile * lanes : (tile + 1) * lanes]
+    quarter = half_cols // 2
+    for line in range(rows // 4):
+        for level in range(levels):
+            for part in range(4):
+                source = ((2 * line + part // 2) * levels + level) * group
+                base = (line * levels + level) * quarter
+                for tile in range(mid // lanes):
+                    place = part * mid + tile * lanes
+                    cat2[base : base + quarter, place : place + lanes] = split_mid[
+                        tile, pl.ds(source + part % 2, quarter, stride=2), :
+                    ]
+    values = layer_norm(cat2[...]).astype(low_type)
+    count, own_count, depth = blocks_ref.shape
+    for index in range(count):
+        blocks_ref[index] = values[:, index * depth : (index + 1) * depth]
+
+    for copy in there + back:
+        copy.wait_send()
+    for copies in (over, across, first, second, third):
+        for copy in copies.values():
+            copy.wait_send()
+
+
+WEIGHT_PIECES = (2, 1, 4)
+
+
+def attend(tokens, qkv_weight, proj_weight, merge_one):
+    rows, slots, width = tokens.shape
+    low, f32 = jnp.bfloat16, jnp.float32
+    levels = slots // (slots // 2)
+    count = lax.axis_size("lon")
+    near = levels * SHIFT_C
+    edge = -(-near // 8) * 8
+    half_cols = slots // levels // 2
+    group = -(-half_cols // 8) * 8
+    cats = rows // 2 * levels * group
+    mid = 4 * merge_one.shape[1]
+    own_count = rows // 4 * levels * (half_cols // 2)
+    whole = pl.BlockSpec(memory_space=pltpu.VMEM)
+    apart = pl.BlockSpec(memory_space=pl.ANY)
+    tall = rows * slots
+    return pl.pallas_call(
+        attend_kernel,
+        out_shape=[
+            jax.ShapeDtypeStruct((rows, slots, width), f32),
+            jax.ShapeDtypeStruct((cats, mid), low),
+            jax.ShapeDtypeStruct((count, own_count, 4 * mid // count), low),
+        ],
+        in_specs=[whole, apart, apart, apart],
+        out_specs=[whole] * 3,
+        scratch_shapes=[
+            pltpu.VMEM((4,) + qkv_weight.shape, low),
+            pltpu.VMEM((proj_weight.shape[0], 4 * proj_weight.shape[1]), low),
+            pltpu.VMEM((4,) + merge_one.shape, low),
+            pltpu.VMEM((rows, edge, width), low),
+            pltpu.VMEM((SHIFT_R, slots, width), low),
+            pltpu.VMEM((rows, edge, width), low),
+            pltpu.VMEM((rows, slots, width), f32),
+            pltpu.VMEM((tall, width), low),
+            pltpu.VMEM((tall, 3 * width), low),
+            pltpu.VMEM((WIN_R * slots, WIN_R * slots), f32),
+            pltpu.VMEM((tall, width), low),
+            pltpu.VMEM((rows, edge, width), low),
+            pltpu.VMEM((SHIFT_R, slots, width), low),
+            pltpu.VMEM((rows, slots, width), f32),
+            pltpu.VMEM((SHIFT_R, slots, width), low),
+            pltpu.VMEM((rows, edge, width), low),
+            pltpu.VMEM((width // 128, rows, slots, 128), f32),
+            pltpu.VMEM((cats, 4 * width), f32),
+            pltpu.VMEM((cats, 4 * width), low),
+            pltpu.VMEM((cats, mid), f32),
+            pltpu.VMEM((mid // 128, cats, 128), f32),
+            pltpu.VMEM((own_count, 4 * mid), f32),
+            pltpu.SemaphoreType.DMA((6,)),
+            pltpu.SemaphoreType.DMA((6,)),
+            pltpu.SemaphoreType.DMA((3,)),
+            pltpu.SemaphoreType.DMA((3, 5 * max(WEIGHT_PIECES))),
+            pltpu.SemaphoreType.DMA((3, 5 * max(WEIGHT_PIECES))),
+        ],
+        compiler_params=pltpu.CompilerParams(
+            collective_id=3, has_side_effects=True, vmem_limit_bytes=40 * 1024 * 1024
+        ),
+    )(tokens, qkv_weight, proj_weight, merge_one)
+
+
+def on_any(
     fine_tokens, qkv_weight, proj_weight, merge_one, merge_two, mlp_in, mlp_out, split_weight
 ):
     levels, rows, cols, width = fine_tokens.shape
@@ -525,6 +885,28 @@
     return (fine_out, mid_out)
 
 
+def on_device(
+    fine_tokens, qkv_weight, proj_weight, merge_one, merge_two, mlp_in, mlp_out, split_weight
+):
+    levels, rows, cols, width = fine_tokens.shape
+    lat_count, count = lax.axis_size("lat"), lax.axis_size("lon")
+    fits = count % 2 == 0 and merge_two.shape[1] % (count * 128) == 0
+    if lat_count != 4 or not fits or rows != 2 * WIN_R or cols != WIN_C or levels != 2:
+        return on_any(
+            fine_tokens, qkv_weight, proj_weight, merge_one, merge_two, mlp_in, mlp_out, split_weight
+        )
+    tokens = fine_tokens.transpose(1, 2, 0, 3).reshape(rows, cols * levels, width)
+    fine, merged1, blocks = attend(tokens, qkv_weight, proj_weight, merge_one)
+    fine_out = fine.reshape(rows, cols, levels, width).transpose(2, 0, 1, 3)
+    pieces = coarse_in_one(blocks, merge_two, mlp_in, mlp_out, split_weight)
+    half_rows, half_cols = rows // 2, cols // 2
+    pieces = pieces.transpose(1, 0, 2).reshape(rows // 4, levels, cols // 4, 2, 2, MID)
+    pieces = pieces.transpose(0, 3, 2, 4, 1, 5).reshape(half_rows, half_cols, levels, MID)
+    merged1 = merged1.reshape(half_rows, levels, -1, MID)[:, :, :half_cols].transpose(0, 2, 1, 3)
+    mid_out = merged1.astype(jnp.float32) + pieces.astype(jnp.float32)
+    return (fine_out, mid_out.transpose(2, 0, 1, 3))
+
+
 def solution(mesh):
     return jax.shard_map(
         on_device,

time: 143 us -> 127 us (0.89); the launches traced: 140 us -> 126 us
  Pallas kernels: 105 us -> 117 us
  matrix products: 10.5 us -> 0 us
  local copies, waits for them, and re-layouts: 13.5 us -> 6.62 us
  other arithmetic: 8.07 us -> 2.01 us
  starting transfers between devices: 1.82 us -> 0 us
    dot_general x7 -> x0, matrix products: 8.06 us -> none  [the longest x4 3.68 us: on_device(): jnp.dot(normed1, part, preferred_element_type=jnp.float32)]
    pallas_call x2 -> x1, Pallas kernels: 34 us -> 40.8 us  [attend(): pl.pallas_call(attend_kernel, out_shape=[jax.ShapeDtypeStruct((rows, slot...]
    pallas_call x1, Pallas kernels: 71.1 us -> 76.3 us  [coarse_in_one(): pl.pallas_call(coarse_kernel, out_shape=jax.ShapeDtypeStruct((count, own_...]
    reduce_sum x6 -> x0, other arithmetic: 3.64 us -> none  [the longest x3 2.04 us: layer_norm(): spread = jnp.mean(shifted * shifted, axis=-1, keepdims=True)]
    slice x5 -> x0, local copies, waits for them, and re-layouts: 3.62 us -> none  [the longest x1 1.11 us: on_device(): fine_tokens[:, SHIFT_R:, SHIFT_C:]]
    sub x1 -> x0, matrix products: 2.43 us -> none  [on_device(): expo = jnp.exp(scores - top)]
    ppermute x3 -> x0, starting transfers between devices: 1.82 us -> none  [lat_swap(): lax.ppermute(value, 'lat', [(index, index ^ mask) for index in range(4)])]
    unnamed x17 -> x8, local copies, waits for them, and re-layouts: 4.59 us -> 3.79 us
  transfers between devices with their start and end apart: 3 -> 0, of which waited for: 0 -> 0; matrix products, arithmetic and copies ran while one was open for 17% -> 0% of each run, Pallas kernels for 9% -> 0%
where the time goes in v1:
time: 127 us; the launch traced here: 126 us
  Pallas kernels  117 us (92%)
  local copies, waits for them, and re-layouts  6.62 us (5%)
  other arithmetic  2.01 us (2%)
    pallas_call x1, Pallas kernels, coarse_in_one(): pl.pallas_call(coarse_kernel, out_shape=jax.ShapeDtypeStruct((count, own_...  76.3 us
    pallas_call x1, Pallas kernels, attend(): pl.pallas_call(attend_kernel, out_shape=[jax.ShapeDtypeStruct((rows, slot...  40.8 us
    unnamed x8, local copies, waits for them, and re-layouts  3.79 us

profile of v1, /device:TPU:0, one launch (start us, length us, event | category | flops | bytes accessed | tf_op | source)
XLA Modules:
  0.0 126.4 jit_solution(6714986304098248377)
XLA Ops:
  0.6 1.1 reshape.19.tok
  1.7 0.0 copy-start
  1.7 1.2 copy-done
  2.9 0.0 copy-start.1
  2.9 1.0 copy-done.1
  3.9 0.0 copy-start.3
  3.9 0.9 copy-done.3
  4.8 40.8 %shard_map.95 = (f32[12,24,512]{2,1,0:T(8,128)S(1)}, bf16[96,1024]{1,0:T(8,128)(2,1)S(1)}, bf16[8,18,512]{2,1,0:T(8,128)(2,1)S(1)}) custom-call(bf16[12,24,512]{2,1,0:T(8,128)(2,1)S(1)} %reshape.19.tok, bf16[512,384]{1,0:T(8,128)(2,1)S(1)} %copy-done.1, bf16[512,128]{1,0:T(8,128)(2,1)S(1)} %copy-done.3, bf16[2048,256]{1,0:T(8,128)(2,1)S(1)} %copy-done), custom_call_target="tpu_custom_call" | custom-call | tf_op jit(solution)/shard_map/pallas_call | solution.py:750
  45.6 0.0 copy-start.2
  45.6 0.7 copy-done.2
  46.3 76.3 %shard_map.96 = bf16[8,18,512]{2,1,0:T(8,128)(2,1)} custom-call(bf16[8,18,512]{2,1,0:T(8,128)(2,1)} %copy-done.2, bf16[512,2048]{1,0:T(8,128)(2,1)} %two_hbm.1, bf16[2048,1024]{1,0:T(8,128)(2,1)} %in_hbm.1, bf16[1024,2048]{1,0:T(8,128)(2,1)} %out_hbm.1, bf16[2048,512]{1,0:T(8,128)(2,1)} %split_hbm.1), custom_call_target="tpu_custom_call" | custom-call | tf_op jit(solution)/shard_map/pallas_call | solution.py:247
  122.6 1.0 convert_bitcast_fusion
  123.6 0.2 copy.14
  123.7 0.2 reshape.23
  124.0 0.2 copy.15
  124.2 1.0 fusion.1
  125.2 1.2 reshape.20
  (1 shorter events, 0.0 us)
Async XLA Ops:
  1.7 1.2 copy-start
  2.9 1.0 copy-start.1
  3.9 0.9 copy-start.3
  45.6 0.7 copy-start.2

commit v2 on v1

--- a/solution.py
+++ b/solution.py
@@ -29,16 +29,21 @@
     return grid.reshape(lev * (rows // 2) * (cols // 2), 4 * width)
 
 
-def coarse_kernel(
+def coarse_steps(
     blocks_ref, two_hbm, in_hbm, out_hbm, split_hbm, pieces_ref,
-    two, w_in, w_out, split, landed, features, sent, summed, own, gathered, normed, act,
-    sent2, summed2, gathered2, cols, sent3, landed3,
-    load_sem, send_sem, recv_sem, relay_send, relay_recv,
+    two, w_in, w_out, split, landed, features, feat, y_sent, y_land, z_sent, z_land, held, own,
+    gathered, normed, act, cols, sent3,
+    load_sem, first_send, first_recv, y_send, y_recv, z_send, z_recv, g_send, g_recv, o_send,
+    o_recv, last_send, last_recv, greet,
 ):
     count = lax.axis_size("lon")
     me = lax.axis_index("lon")
+    chips = count // 2
+    z, y = me // 2, lax.rem(me, 2)
+    partner = me + 1 - 2 * y
     own_count = blocks_ref.shape[1]
-    width = own.shape[1]
+    width = own.shape[-1]
+    low_type, f32 = jnp.bfloat16, jnp.float32
     loads = [
         pltpu.make_async_copy(source, target, load_sem.at[index])
         for index, (source, target) in enumerate(
@@ -47,233 +52,266 @@
     ]
     for load in loads:
         load.start()
-    barrier = pltpu.get_barrier_semaphore()
-
-    def greet(step, carry):
-        peer = lax.rem(me + step, count)
-        pl.semaphore_signal(
-            barrier, inc=1, device_id={"lon": peer}, device_id_type=pl.DeviceIdType.MESH
-        )
-        return carry
-
-    lax.fori_loop(1, count, greet, 0)
-    pl.semaphore_wait(barrier, count - 1)
-
-    def copy_to(phase, peer, source, target):
-        return pltpu.make_async_remote_copy(
-            src_ref=source,
-            dst_ref=target.at[me],
-            send_sem=send_sem.at[phase, peer],
-            recv_sem=recv_sem.at[phase, me],
-            device_id={"lon": peer},
-            device_id_type=pl.DeviceIdType.MESH,
-        )
-
-    def wait_from(phase, target):
-        def body(step, carry):
-            peer = lax.rem(me + step, count)
-            pltpu.make_async_remote_copy(
-                src_ref=target.at[peer],
-                dst_ref=target.at[peer],
-                send_sem=send_sem.at[phase, peer],
-                recv_sem=recv_sem.at[phase, peer],
-                device_id={"lon": peer},
-                device_id_type=pl.DeviceIdType.MESH,
-            ).wait_recv()
-            return carry
-
-        lax.fori_loop(1, count, body, 0)
-
-    def wait_sent(phase, source_of, target):
-        def body(step, carry):
-            peer = lax.rem(me + step, count)
-            copy_to(phase, peer, source_of(peer), target).wait_send()
-            return carry
-
-        lax.fori_loop(1, count, body, 0)
-
-    def scatter_products(phase, left, weight, send, target):
-        def product(peer):
-            cut = pl.ds(pl.multiple_of(peer * width, width), width)
-            return jnp.dot(left[...], weight[:, cut], preferred_element_type=jnp.float32)
-
-        def body(step, carry):
-            peer = lax.rem(me + step, count)
-            send[peer] = product(peer).astype(jnp.bfloat16)
-            copy_to(phase, peer, send.at[peer], target).start()
-            return carry
-
-        lax.fori_loop(1, count, body, 0)
-        total = product(me)
-        wait_from(phase, target)
-
-        def add(step, total):
-            return total + target[lax.rem(me + step, count)].astype(jnp.float32)
-
-        return lax.fori_loop(1, count, add, total)
-
-    chips = count // 2
-    z, y = me // 2, lax.rem(me, 2)
-    partner = me + 1 - 2 * y
-    up, down, over = 0, 1, 2
-
-    def hop(source, target, sent_sem, came_sem, peer):
+    greet()
+    far_first = list(range(2, chips)) + [1] if chips > 2 else list(range(1, chips))
+
+    def level(step):
+        return lax.rem(z + step, chips)
+
+    def remote(source, target, sent, came, peer):
         return pltpu.make_async_remote_copy(
             src_ref=source,
             dst_ref=target,
-            send_sem=sent_sem,
-            recv_sem=came_sem,
+            send_sem=sent,
+            recv_sem=came,
             device_id={"lon": peer},
             device_id_type=pl.DeviceIdType.MESH,
         )
 
-    def relay(phase, target, kind, block, peer):
-        return hop(
-            target.at[block],
-            target.at[block],
-            relay_send.at[phase, kind, block],
-            relay_recv.at[phase, block],
+    def first_copy(peer, source):
+        return remote(
+            blocks_ref.at[peer],
+            landed.at[lax.rem(source, 2), source // 2],
+            first_send.at[peer],
+            first_recv.at[source],
             peer,
         )
 
-    def relays(phase, target, act_on, arriving):
-        pl.when(z < chips - 1)(lambda: act_on(relay(phase, target, up, me, me + 2)))
-        pl.when(z > 0)(lambda: act_on(relay(phase, target, down, me, me - 2)))
-        act_on(relay(phase, target, over, me, partner))
-        for far in range(1, chips):
-
-            @pl.when(z - far >= 0)
-            def _():
-                block = me - 2 * far
-                if arriving:
-                    relay(phase, target, up, block, me - 2).wait_recv()
-                pl.when(z < chips - 1)(
-                    lambda: act_on(relay(phase, target, up, block, me + 2))
-                )
-                act_on(relay(phase, target, over, block, partner))
-
-            @pl.when(z + far < chips)
-            def _():
-                block = me + 2 * far
-                if arriving:
-                    relay(phase, target, down, block, me + 2).wait_recv()
-                pl.when(z > 0)(lambda: act_on(relay(phase, target, down, block, me - 2)))
-                act_on(relay(phase, target, over, block, partner))
-
-    def gather(phase, target):
-        relays(phase, target, lambda copy: copy.start(), True)
-        for row in range(chips):
-            relay(phase, target, over, 2 * row + 1 - y, partner).wait_recv()
-
-    def wait_gather(phase, target):
-        relays(phase, target, lambda copy: copy.wait_send(), False)
-
-    def first(step, carry):
+    def y_copy(phase, chunk, block):
+        return remote(
+            y_sent.at[phase, chunk, block],
+            y_land.at[phase, chunk, block],
+            y_send.at[phase, chunk, block],
+            y_recv.at[phase, chunk, block],
+            partner,
+        )
+
+    def z_copy(phase, chunk, to, source):
+        return remote(
+            z_sent.at[phase, chunk, to],
+            z_land.at[phase, chunk, source],
+            z_send.at[phase, chunk, to],
+            z_recv.at[phase, chunk, source],
+            to * 2 + y,
+        )
+
+    def g_copy(phase, chunk, to, source):
+        place = gathered.at[phase, chunk, source * 2 + y]
+        return remote(
+            place, place, g_send.at[phase, chunk, to], g_recv.at[phase, chunk, source], to * 2 + y
+        )
+
+    def o_copy(phase, chunk, block, side):
+        place = gathered.at[phase, chunk, block * 2 + side]
+        return remote(
+            place, place, o_send.at[phase, chunk, block], o_recv.at[phase, chunk, block], partner
+        )
+
+    def last_copy(peer, source):
+        return remote(
+            sent3.at[lax.rem(peer, 2), peer // 2],
+            pieces_ref.at[source],
+            last_send.at[peer],
+            last_recv.at[source],
+            peer,
+        )
+
+    def product(left, weight, peer):
+        cut = pl.ds(pl.multiple_of(peer * width, width), width)
+        return jnp.dot(left[...], weight[:, cut], preferred_element_type=f32)
+
+    def start_y(phase, chunk, left, weight):
+        for step in far_first + [0]:
+            block = level(step)
+            y_sent[phase, chunk, block] = product(left, weight, block * 2 + 1 - y).astype(low_type)
+            y_copy(phase, chunk, block).start()
+
+    def hold(chunk, left, weight):
+        for step in far_first + [0]:
+            block = level(step)
+            held[chunk, block] = product(left, weight, block * 2 + y)
+
+    def start_z(phase, chunk):
+        for step in far_first:
+            block = level(step)
+            y_copy(phase, chunk, block).wait_recv()
+            total = held[chunk, block] + y_land[phase, chunk, block].astype(f32)
+            z_sent[phase, chunk, block] = total.astype(low_type)
+            z_copy(phase, chunk, block, z).start()
+
+    def finish(phase, chunk):
+        y_copy(phase, chunk, z).wait_recv()
+        total = held[chunk, z] + y_land[phase, chunk, z].astype(f32)
+        for step in range(1, chips):
+            block = level(step)
+            z_copy(phase, chunk, block, block).wait_recv()
+            total = total + z_land[phase, chunk, block].astype(f32)
+        return total
+
+    def spread(phase, chunk, values):
+        gathered[phase, chunk, me] = values.astype(low_type)
+        for step in far_first:
+            g_copy(phase, chunk, level(step), z).start()
+        o_copy(phase, chunk, z, y).start()
+
+    def forward(phase, chunk):
+        for step in range(1, chips):
+            block = level(step)
+            g_copy(phase, chunk, block, block).wait_recv()
+            o_copy(phase, chunk, block, y).start()
+
+    def arrive(phase, chunk):
+        for step in range(chips):
+            o_copy(phase, chunk, level(step), 1 - y).wait_recv()
+
+    for step in range(1, count):
+        first_copy(lax.rem(me + step, count), me).start()
+    landed[y, z] = blocks_ref[me]
+    chunks = (0, 1)
+    for chunk in chunks:
+        for index in range(chips):
+            source = index * 2 + chunk
+            pl.when(source != me)(lambda: first_copy(source, source).wait_recv())
+        for index in range(chips):
+            features[index * own_count : (index + 1) * own_count] = landed[chunk, index].astype(f32)
+        feat[chunk] = features[...].astype(low_type)
+        if chunk == 0:
+            loads[0].wait()
+        start_y(0, chunk, feat.at[chunk], two)
+    for chunk in chunks:
+        hold(chunk, feat.at[chunk], two)
+        start_z(0, chunk)
+    for chunk in chunks:
+        merged = finish(0, chunk)
+        own[chunk] = merged
+        spread(0, chunk, merged)
+    loads[1].wait()
+    loads[2].wait()
+    total_width = count * width
+    tile = min(256, act.shape[-1])
+    for chunk in chunks:
+        forward(0, chunk)
+    for chunk in chunks:
+        arrive(0, chunk)
+        centre = gathered[0, chunk, 0].astype(f32).sum(axis=-1, keepdims=True)
+        for index in range(1, count):
+            centre += gathered[0, chunk, index].astype(f32).sum(axis=-1, keepdims=True)
+        centre = centre / total_width
+        spread_sum = jnp.zeros_like(centre)
+        for index in range(count):
+            shifted = gathered[0, chunk, index].astype(f32) - centre
+            spread_sum += (shifted * shifted).sum(axis=-1, keepdims=True)
+        scale = lax.rsqrt(spread_sum / total_width + 1e-05)
+        for index in range(count):
+            shifted = gathered[0, chunk, index].astype(f32) - centre
+            normed[chunk, :, index * width : (index + 1) * width] = (shifted * scale).astype(
+                low_type
+            )
+
+        def hidden(index, carry):
+            cut = pl.ds(pl.multiple_of(index * tile, tile), tile)
+            values = jnp.dot(normed[chunk], w_in[:, cut], preferred_element_type=f32)
+            act[chunk, :, cut] = jax.nn.gelu(values).astype(low_type)
+            return carry
+
+        lax.fori_loop(0, act.shape[-1] // tile, hidden, 0)
+        start_y(1, chunk, act.at[chunk], w_out)
+    for chunk in chunks:
+        hold(chunk, act.at[chunk], w_out)
+        start_z(1, chunk)
+    for chunk in chunks:
+        spread(1, chunk, own[chunk] + finish(1, chunk))
+    for chunk in chunks:
+        forward(1, chunk)
+    loads[3].wait()
+    for chunk in chunks:
+        arrive(1, chunk)
+        for index in range(count):
+            normed[chunk, :, index * width : (index + 1) * width] = gathered[1, chunk, index]
+        cols[...] = jnp.dot(normed[chunk], split[...], preferred_element_type=f32)
+        for index in range(chips):
+            values = cols[index * own_count : (index + 1) * own_count]
+            sent3[chunk, index] = values.astype(low_type)
+        for step in range(chips):
+            peer = level(step) * 2 + chunk
+            pl.when(peer != me)(lambda: last_copy(peer, me).start())
+    pieces_ref[me] = sent3[y, z]
+    for step in range(1, count):
+        source = lax.rem(me + step, count)
+        last_copy(source, source).wait_recv()
+    for step in range(1, count):
         peer = lax.rem(me + step, count)
-        copy_to(0, peer, blocks_ref.at[peer], landed).start()
-        return carry
-
-    lax.fori_loop(1, count, first, 0)
-    landed[me] = blocks_ref[me]
-    wait_from(0, landed)
-    for index in range(count):
-        features[index * own_count : (index + 1) * own_count] = landed[index].astype(jnp.float32)
-    normed[:, : features.shape[1]] = features[...].astype(jnp.bfloat16)
-    loads[0].wait()
-    merged = scatter_products(1, normed.at[:, : features.shape[1]], two, sent, summed)
-    own[...] = merged
-    gathered[me] = merged.astype(jnp.bfloat16)
-    gather(0, gathered)
-
-    total_width = count * width
-    centre = gathered[0].astype(jnp.float32).sum(axis=-1, keepdims=True)
-    for index in range(1, count):
-        centre += gathered[index].astype(jnp.float32).sum(axis=-1, keepdims=True)
-    centre = centre / total_width
-    spread = jnp.zeros_like(centre)
-    for index in range(count):
-        shifted = gathered[index].astype(jnp.float32) - centre
-        spread += (shifted * shifted).sum(axis=-1, keepdims=True)
-    scale = lax.rsqrt(spread / total_width + 1e-05)
-    for index in range(count):
-        shifted = gathered[index].astype(jnp.float32) - centre
-        normed[:, index * width : (index + 1) * width] = (shifted * scale).astype(jnp.bfloat16)
-    loads[1].wait()
-
-    tile = min(256, act.shape[1])
-
-    def hidden(index, carry):
-        cut = pl.ds(pl.multiple_of(index * tile, tile), tile)
-        values = jnp.dot(normed[...], w_in[:, cut], preferred_element_type=jnp.float32)
-        act[:, cut] = jax.nn.gelu(values).astype(jnp.bfloat16)
-        return carry
-
-    lax.fori_loop(0, act.shape[1] // tile, hidden, 0)
-    loads[2].wait()
-    mlp = scatter_products(3, act, w_out, sent2, summed2)
-    gathered2[me] = (own[...] + mlp).astype(jnp.bfloat16)
-    gather(1, gathered2)
-    for index in range(count):
-        normed[:, index * width : (index + 1) * width] = gathered2[index]
-    loads[3].wait()
-    cols[...] = jnp.dot(normed[...], split[...], preferred_element_type=jnp.float32)
-    for index in range(count):
-        sent3[index] = cols[index * own_count : (index + 1) * own_count].astype(jnp.bfloat16)
-
-    def last(step, carry):
-        peer = lax.rem(me + step, count)
-        copy_to(5, peer, sent3.at[peer], landed3).start()
-        return carry
-
-    lax.fori_loop(1, count, last, 0)
-    landed3[me] = sent3[me]
-    wait_from(5, landed3)
-    pieces_ref[...] = landed3[...]
-    wait_sent(0, lambda peer: blocks_ref.at[peer], landed)
-    wait_sent(1, lambda peer: sent.at[peer], summed)
-    wait_gather(0, gathered)
-    wait_sent(3, lambda peer: sent2.at[peer], summed2)
-    wait_gather(1, gathered2)
-    wait_sent(5, lambda peer: sent3.at[peer], landed3)
+        first_copy(peer, me).wait_send()
+        last_copy(peer, me).wait_send()
+    for phase in (0, 1):
+        for chunk in chunks:
+            for step in range(chips):
+                y_copy(phase, chunk, level(step)).wait_send()
+                o_copy(phase, chunk, level(step), y).wait_send()
+                if step > 0:
+                    z_copy(phase, chunk, level(step), z).wait_send()
+                    g_copy(phase, chunk, level(step), z).wait_send()
+
+
+def coarse_scratch(count, own_count, depth, merge_two, mlp_in, mlp_out, split_weight):
+    low, f32 = jnp.bfloat16, jnp.float32
+    chips = count // 2
+    tokens, top = chips * own_count, merge_two.shape[1]
+    width, hidden, split_width = top // count, mlp_in.shape[1], split_weight.shape[1]
+    dma = pltpu.SemaphoreType.DMA
+    return [
+        pltpu.VMEM(merge_two.shape, low),
+        pltpu.VMEM(mlp_in.shape, low),
+        pltpu.VMEM(mlp_out.shape, low),
+        pltpu.VMEM(split_weight.shape, low),
+        pltpu.VMEM((2, chips, own_count, depth), low),
+        pltpu.VMEM((tokens, depth), f32),
+        pltpu.VMEM((2, tokens, depth), low),
+        pltpu.VMEM((2, 2, chips, tokens, width), low),
+        pltpu.VMEM((2, 2, chips, tokens, width), low),
+        pltpu.VMEM((2, 2, chips, tokens, width), low),
+        pltpu.VMEM((2, 2, chips, tokens, width), low),
+        pltpu.VMEM((2, chips, tokens, width), f32),
+        pltpu.VMEM((2, tokens, width), f32),
+        pltpu.VMEM((2, 2, count, tokens, width), low),
+        pltpu.VMEM((2, tokens, top), low),
+        pltpu.VMEM((2, tokens, hidden), low),
+        pltpu.VMEM((tokens, split_width), f32),
+        pltpu.VMEM((2, chips, own_count, split_width), low),
+        dma((4,)),
+        dma((count,)),
+        dma((count,)),
+    ] + [dma((2, 2, chips)) for _ in range(8)] + [dma((count,)), dma((count,))]
+
+
+def coarse_kernel(*refs):
+    count = lax.axis_size("lon")
+    me = lax.axis_index("lon")
+
+    def greet():
+        barrier = pltpu.get_barrier_semaphore()
+        for step in range(1, count):
+            peer = lax.rem(me + step, count)
+            pl.semaphore_signal(
+                barrier, inc=1, device_id={"lon": peer}, device_id_type=pl.DeviceIdType.MESH
+            )
+        pl.semaphore_wait(barrier, count - 1)
+
+    coarse_steps(*refs, greet)
 
 
 def coarse_in_one(blocks, merge_two, mlp_in, mlp_out, split_weight):
     count, own_count, depth = blocks.shape
-    tokens, top = count * own_count, merge_two.shape[1]
-    width, hidden, split_width = top // count, mlp_in.shape[1], split_weight.shape[1]
-    low = jnp.bfloat16
     whole = pl.BlockSpec(memory_space=pltpu.VMEM)
     apart = pl.BlockSpec(memory_space=pl.ANY)
     return pl.pallas_call(
         coarse_kernel,
-        out_shape=jax.ShapeDtypeStruct((count, own_count, split_width), low),
+        out_shape=jax.ShapeDtypeStruct((count, own_count, split_weight.shape[1]), jnp.bfloat16),
         in_specs=[whole, apart, apart, apart, apart],
         out_specs=whole,
-        scratch_shapes=[
-            pltpu.VMEM(merge_two.shape, low),
-            pltpu.VMEM(mlp_in.shape, low),
-            pltpu.VMEM(mlp_out.shape, low),
-            pltpu.VMEM(split_weight.shape, low),
-            pltpu.VMEM((count, own_count, depth), low),
-            pltpu.VMEM((tokens, depth), jnp.float32),
-            pltpu.VMEM((count, tokens, width), low),
-            pltpu.VMEM((count, tokens, width), low),
-            pltpu.VMEM((tokens, width), jnp.float32),
-            pltpu.VMEM((count, tokens, width), low),
-            pltpu.VMEM((tokens, top), low),
-            pltpu.VMEM((tokens, hidden), low),
-            pltpu.VMEM((count, tokens, width), low),
-            pltpu.VMEM((count, tokens, width), low),
-            pltpu.VMEM((count, tokens, width), low),
-            pltpu.VMEM((tokens, split_width), jnp.float32),
-            pltpu.VMEM((count, own_count, split_width), low),
-            pltpu.VMEM((count, own_count, split_width), low),
-            pltpu.SemaphoreType.DMA((4,)),
-            pltpu.SemaphoreType.DMA((6, count)),
-            pltpu.SemaphoreType.DMA((6, count)),
-            pltpu.SemaphoreType.DMA((2, 3, count)),
-            pltpu.SemaphoreType.DMA((2, count)),
-        ],
+        scratch_shapes=coarse_scratch(
+            count, own_count, depth, merge_two, mlp_in, mlp_out, split_weight
+        ),
         compiler_params=pltpu.CompilerParams(
             collective_id=0, has_side_effects=True, vmem_limit_bytes=60 * 1024 * 1024
         ),
@@ -786,7 +824,7 @@
             pltpu.SemaphoreType.DMA((3, 5 * max(WEIGHT_PIECES))),
         ],
         compiler_params=pltpu.CompilerParams(
-            collective_id=3, has_side_effects=True, vmem_limit_bytes=40 * 1024 * 1024
+            collective_id=3, has_side_effects=True, vmem_limit_bytes=60 * 1024 * 1024
         ),
     )(tokens, qkv_weight, proj_weight, merge_one)
 

time: 127 us -> 108 us (0.85)
  Pallas kernels: 117 us -> 101 us
  local copies, waits for them, and re-layouts: 6.62 us -> 3.56 us
    pallas_call x1, Pallas kernels: 76.3 us -> 58.3 us  [coarse_in_one(): pl.pallas_call(coarse_kernel, out_shape=jax.ShapeDtypeStruct((count, own_...]
    unnamed x8 -> x4, local copies, waits for them, and re-layouts: 3.79 us -> 0.01 us
    pallas_call x1, Pallas kernels: 40.8 us -> 42.9 us  [attend(): pl.pallas_call(attend_kernel, out_shape=[jax.ShapeDtypeStruct((rows, slot...]
where the time goes in v2:
time: 108 us
  Pallas kernels  101 us (94%)
  local copies, waits for them, and re-layouts  3.56 us (3%)
  other arithmetic  2.07 us (2%)
    pallas_call x1, Pallas kernels, coarse_in_one(): pl.pallas_call(coarse_kernel, out_shape=jax.ShapeDtypeStruct((count, own_...  58.3 us
    pallas_call x1, Pallas kernels, attend(): pl.pallas_call(attend_kernel, out_shape=[jax.ShapeDtypeStruct((rows, slot...  42.9 us

profile of v2, /device:TPU:0, one launch (start us, length us, event | category | flops | bytes accessed | tf_op | source)
XLA Modules:
  0.0 107.6 jit_solution(1857384723823846685)
XLA Ops:
  0.6 1.8 %reshape.19.tok = bf16[12,24,512]{2,1,0:T(8,128)(2,1)} reshape(bf16[12,12,2,512]{3,2,1,0:T(2,128)(2,1)} %bitcast.18) | data formatting | bytes 589824 | tf_op jit(solution)/shard_map/reshape | solution.py:936
  2.4 42.9 %shard_map.95 = (f32[12,24,512]{2,1,0:T(8,128)}, bf16[96,1024]{1,0:T(8,128)(2,1)}, bf16[8,18,512]{2,1,0:T(8,128)(2,1)}) custom-call(bf16[12,24,512]{2,1,0:T(8,128)(2,1)} %reshape.19.tok, bf16[512,384]{1,0:T(8,128)(2,1)} %qkv_hbm.1, bf16[512,128]{1,0:T(8,128)(2,1)} %proj_hbm.1, bf16[2048,256]{1,0:T(8,128)(2,1)} %merge_hbm.1), custom_call_target="tpu_custom_call" | custom-call | tf_op jit(solution)/shard_map/pallas_call | solution.py:788
  45.4 0.0 copy-start.1
  45.4 58.3 %shard_map.96 = bf16[8,18,512]{2,1,0:T(8,128)(2,1)} custom-call(bf16[8,18,512]{2,1,0:T(8,128)(2,1)} %get-tuple-element.7.refs_0_, bf16[512,2048]{1,0:T(8,128)(2,1)} %refs_1_.1, bf16[2048,1024]{1,0:T(8,128)(2,1)} %refs_2_.1, bf16[1024,2048]{1,0:T(8,128)(2,1)} %refs_3_.1, bf16[2048,512]{1,0:T(8,128)(2,1)} %refs_4_.1), custom_call_target="tpu_custom_call" | custom-call | tf_op jit(solution)/shard_map/pallas_call | solution.py:307
  103.7 0.0 copy-start
  103.7 1.0 convert_bitcast_fusion
  104.7 0.2 copy.14
  104.9 0.2 reshape.23
  105.1 0.2 copy.15
  105.3 0.0 copy-done.1
  105.4 1.0 fusion.1
  106.4 0.0 copy-done
  106.4 1.2 %reshape.20 = f32[12,12,2,512]{3,2,1,0:T(2,128)} reshape(f32[12,24,512]{2,1,0:T(8,128)S(1)} %copy-done) | data formatting | bytes 1179648 | tf_op jit(solution)/shard_map/reshape | solution.py:938
  (1 shorter events, 0.0 us)
Async XLA Ops:
  45.4 60.0 %copy-start.1 = (bf16[96,1024]{1,0:T(8,128)(2,1)S(1)}, bf16[96,1024]{1,0:T(8,128)(2,1)}, u32[]{:S(2)}) copy-start(bf16[96,1024]{1,0:T(8,128)(2,1)} %get-tuple-element.6) | copy-start | bytes 589828
  103.7 2.7 %copy-start = (f32[12,24,512]{2,1,0:T(8,128)S(1)}, f32[12,24,512]{2,1,0:T(8,128)}, u32[]{:S(2)}) copy-start(f32[12,24,512]{2,1,0:T(8,128)} %get-tuple-element.5) | copy-start | bytes 1769476

commit v3 on v2

--- a/solution.py
+++ b/solution.py
@@ -29,12 +29,19 @@
     return grid.reshape(lev * (rows // 2) * (cols // 2), 4 * width)
 
 
+def coarse_loads(sources, targets, sems):
+    return [
+        pltpu.make_async_copy(source, target, sems.at[index])
+        for index, (source, target) in enumerate(zip(sources, targets))
+    ]
+
+
 def coarse_steps(
     blocks_ref, two_hbm, in_hbm, out_hbm, split_hbm, pieces_ref,
     two, w_in, w_out, split, landed, features, feat, y_sent, y_land, z_sent, z_land, held, own,
     gathered, normed, act, cols, sent3,
     load_sem, first_send, first_recv, y_send, y_recv, z_send, z_recv, g_send, g_recv, o_send,
-    o_recv, last_send, last_recv, greet,
+    o_recv, last_send, last_recv,
 ):
     count = lax.axis_size("lon")
     me = lax.axis_index("lon")
@@ -44,15 +51,7 @@
     own_count = blocks_ref.shape[1]
     width = own.shape[-1]
     low_type, f32 = jnp.bfloat16, jnp.float32
-    loads = [
-        pltpu.make_async_copy(source, target, load_sem.at[index])
-        for index, (source, target) in enumerate(
-            ((two_hbm, two), (in_hbm, w_in), (out_hbm, w_out), (split_hbm, split))
-        )
-    ]
-    for load in loads:
-        load.start()
-    greet()
+    loads = coarse_loads((two_hbm, in_hbm, out_hbm, split_hbm), (two, w_in, w_out, split), load_sem)
     far_first = list(range(2, chips)) + [1] if chips > 2 else list(range(1, chips))
 
     def level(step):
@@ -284,40 +283,6 @@
     ] + [dma((2, 2, chips)) for _ in range(8)] + [dma((count,)), dma((count,))]
 
 
-def coarse_kernel(*refs):
-    count = lax.axis_size("lon")
-    me = lax.axis_index("lon")
-
-    def greet():
-        barrier = pltpu.get_barrier_semaphore()
-        for step in range(1, count):
-            peer = lax.rem(me + step, count)
-            pl.semaphore_signal(
-                barrier, inc=1, device_id={"lon": peer}, device_id_type=pl.DeviceIdType.MESH
-            )
-        pl.semaphore_wait(barrier, count - 1)
-
-    coarse_steps(*refs, greet)
-
-
-def coarse_in_one(blocks, merge_two, mlp_in, mlp_out, split_weight):
-    count, own_count, depth = blocks.shape
-    whole = pl.BlockSpec(memory_space=pltpu.VMEM)
-    apart = pl.BlockSpec(memory_space=pl.ANY)
-    return pl.pallas_call(
-        coarse_kernel,
-        out_shape=jax.ShapeDtypeStruct((count, own_count, split_weight.shape[1]), jnp.bfloat16),
-        in_specs=[whole, apart, apart, apart, apart],
-        out_specs=whole,
-        scratch_shapes=coarse_scratch(
-            count, own_count, depth, merge_two, mlp_in, mlp_out, split_weight
-        ),
-        compiler_params=pltpu.CompilerParams(
-            collective_id=0, has_side_effects=True, vmem_limit_bytes=60 * 1024 * 1024
-        ),
-    )(blocks, merge_two, mlp_in, mlp_out, split_weight)
-
-
 def coarse_apart(normed2, merge_two, mlp_in, mlp_out, split_weight):
     own_count = normed2.shape[0]
     feature_parts = lax.all_to_all(normed2, "lon", split_axis=1, concat_axis=0, tiled=True)
@@ -470,10 +435,10 @@
 
 
 def attend_kernel(
-    tok, qkv_hbm, proj_hbm, merge_hbm, fine_ref, merged_ref, blocks_ref,
+    tok, qkv_hbm, proj_hbm, merge_hbm, fine_ref, blocks_ref,
     wq, wp, wm, low, came_row, came_low, packed, normed, qkv, bias, heads, low_back, row_back,
     attn, back_row, back_low, split_fine, cat, cat_low, parts, split_mid, cat2,
-    halo_send, halo_recv, own_sem, weight_send, weight_recv,
+    halo_send, halo_recv, own_sem, weight_send, weight_recv, start_loads,
 ):
     lat_count, lon_count = lax.axis_size("lat"), lax.axis_size("lon")
     row, col = lax.axis_index("lat"), lax.axis_index("lon")
@@ -495,9 +460,13 @@
     far = lax.rem(other_core + 2, 4)
     side = lax.rem(col, 2)
     pair = col + 1 - 2 * side
+    high_side = lax.rem(col // 2, 2)
+    high_pair = col + 2 - 4 * high_side
+    sides, pairs = (side, side, high_side), (pair, pair, high_pair)
     low[...] = tok[...].astype(f32)[:, :edge].astype(low_type)
     cat[...] = jnp.zeros_like(cat)
-    partners = beside(1) + beside(-1) + ((other_core, col), (other_chip, col), (row, pair))
+    partners = beside(1) + beside(-1) + ((other_core, col), (other_chip, col))
+    partners += tuple((row, lax.rem(col + step, lon_count)) for step in range(1, lon_count))
     barrier = pltpu.get_barrier_semaphore()
     for partner in partners:
         pl.semaphore_signal(barrier, inc=1, device_id=partner, device_id_type=mesh)
@@ -538,8 +507,8 @@
         for number in range(counts[index]):
             over[index, number] = send(
                 index, 0, number,
-                piece(shards[index], index, side, number),
-                piece(whole(index, row), index, side, number),
+                piece(shards[index], index, sides[index], number),
+                piece(whole(index, row), index, sides[index], number),
                 (other_chip, col),
             )
 
@@ -552,13 +521,13 @@
 
     def pass_on(index, number):
         over[index, number].wait_recv()
-        held = piece(whole(index, other_chip), index, side, number)
-        first[index, number] = send(index, 2, number, held, held, (row, pair))
+        held = piece(whole(index, other_chip), index, sides[index], number)
+        first[index, number] = send(index, 2, number, held, held, (row, pairs[index]))
         second[index, number] = send(index, 3, number, held, held, (other_core, col))
 
     def pass_last(index, number):
         first[index, number].wait_recv()
-        held = piece(whole(index, other_chip), index, 1 - side, number)
+        held = piece(whole(index, other_chip), index, 1 - sides[index], number)
         third[index, number] = send(index, 4, number, held, held, (other_core, col))
 
     def wait_far(index):
@@ -583,13 +552,14 @@
         halo(0, low.at[SHIFT_R:], came_low.at[SHIFT_R:], before[1]),
         halo(1, low.at[:SHIFT_R], came_low.at[:SHIFT_R], before[2]),
     ]
+    there.append(halo(2, tok.at[:SHIFT_R], came_row, before[0]))
     send_over(0)
-    there.append(halo(2, tok.at[:SHIFT_R], came_row, before[0]))
     send_across(0)
     send_over(1)
     send_across(1)
     send_over(2)
     send_across(2)
+    start_loads()
 
     slot = lax.broadcasted_iota(jnp.int32, (1, edge, width), 1)
     tokens = WIN_R * slots
@@ -673,11 +643,10 @@
     for win in range(wins):
         attend(win)
         if win == 0:
-            for number in range(counts[1]):
-                pass_last(1, number)
-        pass_on(2, win + 1)
-        pass_last(2, win)
-
+            pass_on(2, 1)
+
+    for number in range(counts[1]):
+        pass_last(1, number)
     own[1].wait()
     across[1].wait_recv()
     wait_far(1)
@@ -695,8 +664,11 @@
         halo(4, low_back.at[kept:], back_low.at[:SHIFT_R], after[2]),
         halo(5, row_back, back_row, after[0]),
     ]
-    for number in range(wins + 1, counts[2]):
+    pass_on(2, 2)
+    pass_last(2, 0)
+    for number in range(3, counts[2]):
         pass_on(2, number)
+    pass_last(2, 1)
     for copy in back:
         copy.wait_recv()
 
@@ -723,7 +695,7 @@
                     cat[base : base + half_cols, place : place + lanes] = split_fine[
                         tile, 2 * line + part // 2, pl.ds(start, half_cols, stride=2 * levels), :
                     ]
-    for number in range(wins, counts[2]):
+    for number in range(2, counts[2]):
         pass_last(2, number)
     cat_low[...] = layer_norm(cat[...]).astype(low_type)
     wide = merge_hbm.shape[1]
@@ -740,7 +712,6 @@
     merge(other_chip)
     wait_far(2)
     merge(far)
-    merged_ref[...] = parts[...].astype(low_type)
     mid = parts.shape[1]
     for tile in range(mid // lanes):
         split_mid[tile] = parts[:, tile * lanes : (tile + 1) * lanes]
@@ -760,17 +731,84 @@
     for index in range(count):
         blocks_ref[index] = values[:, index * depth : (index + 1) * depth]
 
-    for copy in there + back:
-        copy.wait_send()
-    for copies in (over, across, first, second, third):
-        for copy in copies.values():
+
+    def drain():
+        for copy in there + back:
             copy.wait_send()
+        for copies in (over, across, first, second, third):
+            for copy in copies.values():
+                copy.wait_send()
+
+    return drain
 
 
 WEIGHT_PIECES = (2, 1, 4)
 
 
-def attend(tokens, qkv_weight, proj_weight, merge_one):
+def count_up(values, size, total):
+    found = jnp.zeros_like(values)
+    for step in range(size, total, size):
+        found += (values >= step).astype(jnp.int32)
+    return found
+
+
+def place_pieces(parts, pieces, mid_ref, half_rows, half_cols, levels):
+    low, f32 = jnp.bfloat16, jnp.float32
+    total, mid = mid_ref.shape
+    held = parts.shape[0]
+    group = held // (half_rows * levels)
+    target = lax.broadcasted_iota(jnp.int32, (total, held), 0)
+    source = lax.broadcasted_iota(jnp.int32, (total, held), 1)
+    line = count_up(source, group, held)
+    column = source - line * group
+    row = count_up(line, levels, half_rows * levels)
+    level = line - row * levels
+    match = (target == (row * half_cols + column) * levels + level) & (column < half_cols)
+    chosen = jnp.where(match, 1.0, 0.0).astype(low)
+    mid_ref[...] = jnp.dot(chosen, parts[...].astype(low), preferred_element_type=f32)
+    count, own_count, wide = pieces.shape
+    quarter = half_cols // 2
+    target = lax.broadcasted_iota(jnp.int32, (total, own_count), 0)
+    source = lax.broadcasted_iota(jnp.int32, (total, own_count), 1)
+    line = count_up(source, quarter, own_count)
+    column = source - line * quarter
+    row = count_up(line, levels, own_count)
+    level = line - row * levels
+    blocks = count // 4
+    for part in range(4):
+        place = ((2 * row + part // 2) * half_cols + 2 * column + part % 2) * levels + level
+        chosen = jnp.where(target == place, 1.0, 0.0).astype(low)
+        for block in range(blocks):
+            cut = slice(block * wide, (block + 1) * wide)
+            mid_ref[:, cut] += jnp.dot(
+                chosen, pieces[part * blocks + block], preferred_element_type=f32
+            )
+
+
+def whole_kernel(attend_count, half_rows, half_cols, levels, *refs):
+    ins, weights, outs, rest = refs[:4], refs[4:8], refs[8:10], refs[10:]
+    fine_ref, mid_ref = outs
+    blocks, pieces = rest[:2]
+    attend_refs, coarse_refs = rest[2 : 2 + attend_count], rest[2 + attend_count :]
+    load_sem = coarse_refs[18]
+
+    def start_loads():
+        for load in coarse_loads(weights, coarse_refs[:4], load_sem):
+            load.start()
+
+    drain = attend_kernel(*ins, fine_ref, blocks, *attend_refs, start_loads)
+    coarse_steps(blocks, *weights, pieces, *coarse_refs)
+    parts = attend_refs[PARTS_AT]
+    place_pieces(parts, pieces, mid_ref, half_rows, half_cols, levels)
+    drain()
+
+
+PARTS_AT = 19
+
+
+def whole_block(
+    tokens, qkv_weight, proj_weight, merge_one, merge_two, mlp_in, mlp_out, split_weight
+):
     rows, slots, width = tokens.shape
     low, f32 = jnp.bfloat16, jnp.float32
     levels = slots // (slots // 2)
@@ -785,48 +823,58 @@
     whole = pl.BlockSpec(memory_space=pltpu.VMEM)
     apart = pl.BlockSpec(memory_space=pl.ANY)
     tall = rows * slots
+    depth = 4 * mid // count
+    attend_scratch = [
+        pltpu.VMEM((4,) + qkv_weight.shape, low),
+        pltpu.VMEM((proj_weight.shape[0], 4 * proj_weight.shape[1]), low),
+        pltpu.VMEM((4,) + merge_one.shape, low),
+        pltpu.VMEM((rows, edge, width), low),
+        pltpu.VMEM((SHIFT_R, slots, width), low),
+        pltpu.VMEM((rows, edge, width), low),
+        pltpu.VMEM((rows, slots, width), f32),
+        pltpu.VMEM((tall, width), low),
+        pltpu.VMEM((tall, 3 * width), low),
+        pltpu.VMEM((WIN_R * slots, WIN_R * slots), f32),
+        pltpu.VMEM((tall, width), low),
+        pltpu.VMEM((rows, edge, width), low),
+        pltpu.VMEM((SHIFT_R, slots, width), low),
+        pltpu.VMEM((rows, slots, width), f32),
+        pltpu.VMEM((SHIFT_R, slots, width), low),
+        pltpu.VMEM((rows, edge, width), low),
+        pltpu.VMEM((width // 128, rows, slots, 128), f32),
+        pltpu.VMEM((cats, 4 * width), f32),
+        pltpu.VMEM((cats, 4 * width), low),
+        pltpu.VMEM((cats, mid), f32),
+        pltpu.VMEM((mid // 128, cats, 128), f32),
+        pltpu.VMEM((own_count, 4 * mid), f32),
+        pltpu.SemaphoreType.DMA((6,)),
+        pltpu.SemaphoreType.DMA((6,)),
+        pltpu.SemaphoreType.DMA((3,)),
+        pltpu.SemaphoreType.DMA((3, 5 * max(WEIGHT_PIECES))),
+        pltpu.SemaphoreType.DMA((3, 5 * max(WEIGHT_PIECES))),
+    ]
     return pl.pallas_call(
-        attend_kernel,
+        functools.partial(
+            whole_kernel, len(attend_scratch), rows // 2, half_cols, levels
+        ),
         out_shape=[
             jax.ShapeDtypeStruct((rows, slots, width), f32),
-            jax.ShapeDtypeStruct((cats, mid), low),
-            jax.ShapeDtypeStruct((count, own_count, 4 * mid // count), low),
+            jax.ShapeDtypeStruct((rows // 2 * half_cols * levels, mid), f32),
         ],
-        in_specs=[whole, apart, apart, apart],
-        out_specs=[whole] * 3,
+        in_specs=[whole] + [apart] * 7,
+        out_specs=[whole] * 2,
         scratch_shapes=[
-            pltpu.VMEM((4,) + qkv_weight.shape, low),
-            pltpu.VMEM((proj_weight.shape[0], 4 * proj_weight.shape[1]), low),
-            pltpu.VMEM((4,) + merge_one.shape, low),
-            pltpu.VMEM((rows, edge, width), low),
-            pltpu.VMEM((SHIFT_R, slots, width), low),
-            pltpu.VMEM((rows, edge, width), low),
-            pltpu.VMEM((rows, slots, width), f32),
-            pltpu.VMEM((tall, width), low),
-            pltpu.VMEM((tall, 3 * width), low),
-            pltpu.VMEM((WIN_R * slots, WIN_R * slots), f32),
-            pltpu.VMEM((tall, width), low),
-            pltpu.VMEM((rows, edge, width), low),
-            pltpu.VMEM((SHIFT_R, slots, width), low),
-            pltpu.VMEM((rows, slots, width), f32),
-            pltpu.VMEM((SHIFT_R, slots, width), low),
-            pltpu.VMEM((rows, edge, width), low),
-            pltpu.VMEM((width // 128, rows, slots, 128), f32),
-            pltpu.VMEM((cats, 4 * width), f32),
-            pltpu.VMEM((cats, 4 * width), low),
-            pltpu.VMEM((cats, mid), f32),
-            pltpu.VMEM((mid // 128, cats, 128), f32),
-            pltpu.VMEM((own_count, 4 * mid), f32),
-            pltpu.SemaphoreType.DMA((6,)),
-            pltpu.SemaphoreType.DMA((6,)),
-            pltpu.SemaphoreType.DMA((3,)),
-            pltpu.SemaphoreType.DMA((3, 5 * max(WEIGHT_PIECES))),
-            pltpu.SemaphoreType.DMA((3, 5 * max(WEIGHT_PIECES))),
-        ],
+            pltpu.VMEM((count, own_count, depth), low),
+            pltpu.VMEM((count, own_count, split_weight.shape[1]), low),
+        ]
+        + attend_scratch
+        + coarse_scratch(count, own_count, depth, merge_two, mlp_in, mlp_out, split_weight),
         compiler_params=pltpu.CompilerParams(
-            collective_id=3, has_side_effects=True, vmem_limit_bytes=60 * 1024 * 1024
+            collective_id=3, has_side_effects=True, vmem_limit_bytes=62 * 1024 * 1024
         ),
-    )(tokens, qkv_weight, proj_weight, merge_one)
+    )(
+        tokens, qkv_weight, proj_weight, merge_one, merge_two, mlp_in, mlp_out, split_weight
+    )
 
 
 def on_any(
@@ -910,13 +958,7 @@
         merged1 = merged1.astype(jnp.bfloat16)
     merged1 = merged1.reshape(levels, rows // 2, cols // 2, MID)
     normed2 = layer_norm(cat_four(merged1.astype(jnp.float32))).astype(jnp.bfloat16)
-    count = lax.axis_size("lon")
-    if count % 2 == 0 and merge_two.shape[1] % (count * 128) == 0:
-        blocks = normed2.reshape(normed2.shape[0], count, -1).transpose(1, 0, 2)
-        pieces = coarse_in_one(blocks, merge_two, mlp_in, mlp_out, split_weight)
-        pieces = pieces.transpose(1, 0, 2)
-    else:
-        pieces = coarse_apart(normed2, merge_two, mlp_in, mlp_out, split_weight)
+    pieces = coarse_apart(normed2, merge_two, mlp_in, mlp_out, split_weight)
     pieces = pieces.reshape(levels, rows // 4, cols // 4, 2, 2, MID).transpose(0, 1, 3, 2, 4, 5)
     pieces = pieces.reshape(levels, rows // 2, cols // 2, MID)
     mid_out = merged1.astype(jnp.float32) + pieces.astype(jnp.float32)
@@ -928,21 +970,18 @@
 ):
     levels, rows, cols, width = fine_tokens.shape
     lat_count, count = lax.axis_size("lat"), lax.axis_size("lon")
-    fits = count % 2 == 0 and merge_two.shape[1] % (count * 128) == 0
+    fits = count % 4 == 0 and merge_two.shape[1] % (count * 128) == 0
     if lat_count != 4 or not fits or rows != 2 * WIN_R or cols != WIN_C or levels != 2:
         return on_any(
             fine_tokens, qkv_weight, proj_weight, merge_one, merge_two, mlp_in, mlp_out, split_weight
         )
     tokens = fine_tokens.transpose(1, 2, 0, 3).reshape(rows, cols * levels, width)
-    fine, merged1, blocks = attend(tokens, qkv_weight, proj_weight, merge_one)
+    fine, mid = whole_block(
+        tokens, qkv_weight, proj_weight, merge_one, merge_two, mlp_in, mlp_out, split_weight
+    )
     fine_out = fine.reshape(rows, cols, levels, width).transpose(2, 0, 1, 3)
-    pieces = coarse_in_one(blocks, merge_two, mlp_in, mlp_out, split_weight)
-    half_rows, half_cols = rows // 2, cols // 2
-    pieces = pieces.transpose(1, 0, 2).reshape(rows // 4, levels, cols // 4, 2, 2, MID)
-    pieces = pieces.transpose(0, 3, 2, 4, 1, 5).reshape(half_rows, half_cols, levels, MID)
-    merged1 = merged1.reshape(half_rows, levels, -1, MID)[:, :, :half_cols].transpose(0, 2, 1, 3)
-    mid_out = merged1.astype(jnp.float32) + pieces.astype(jnp.float32)
-    return (fine_out, mid_out.transpose(2, 0, 1, 3))
+    mid_out = mid.reshape(rows // 2, cols // 2, levels, MID).transpose(2, 0, 1, 3)
+    return (fine_out, mid_out)
 
 
 def solution(mesh):

time: 108 us -> 102 us (0.944)
  Pallas kernels: 101 us -> 94.8 us
  local copies, waits for them, and re-layouts: 3.56 us -> 5.85 us
  other arithmetic: 2.07 us -> 0 us
    pallas_call x2 -> x1, Pallas kernels: 101 us -> 94.8 us  [whole_block(): pl.pallas_call(functools.partial(whole_kernel, len(attend_scratch), rows...]
    reshape x0 -> x1, local copies, waits for them, and re-layouts: none -> 1.84 us  [on_device(): mid.reshape(rows // 2, cols // 2, levels, MID).transpose(2, 0, 1, 3)]
where the time goes in v3:
time: 102 us; the launch traced here: 101 us
  Pallas kernels  94.8 us (93%)
  local copies, waits for them, and re-layouts  5.85 us (6%)
    pallas_call x1, Pallas kernels, whole_block(): pl.pallas_call(functools.partial(whole_kernel, len(attend_scratch), rows...  94.8 us
    reshape x1, local copies, waits for them, and re-layouts, on_device(): fine_out = fine.reshape(rows, cols, levels, width).transpose(2, 0, 1, 3)  2.22 us

profile of v3, /device:TPU:0, one launch (start us, length us, event | category | flops | bytes accessed | tf_op | source)
XLA Modules:
  0.0 101.3 jit_solution(6704675758390328322)
XLA Ops:
  0.6 1.8 %reshape.13.refs_0_ = bf16[12,24,512]{2,1,0:T(8,128)(2,1)} reshape(bf16[12,12,2,512]{3,2,1,0:T(2,128)(2,1)} %bitcast.4) | data formatting | bytes 589824 | tf_op jit(solution)/shard_map/reshape | solution.py:978
  2.4 94.8 %shard_map.95 = (f32[12,24,512]{2,1,0:T(8,128)}, f32[72,1024]{1,0:T(8,128)}) custom-call(bf16[12,24,512]{2,1,0:T(8,128)(2,1)} %reshape.13.refs_0_, bf16[512,384]{1,0:T(8,128)(2,1)} %refs_1_.1, bf16[512,128]{1,0:T(8,128)(2,1)} %refs_2_.1, bf16[2048,256]{1,0:T(8,128)(2,1)} %refs_3_.1, bf16[512,2048]{1,0:T(8,128)(2,1)} %refs_4_.1, bf16[2048,1024]{1,0:T(8,128)(2,1)} %refs_5_.1, ...), custom_call_target="tpu_custom_call" | custom-call | tf_op jit(solution)/shard_map/pallas_call | solution.py:856
  97.2 2.2 %reshape.14 = f32[12,12,2,512]{3,2,1,0:T(2,128)} reshape(f32[12,24,512]{2,1,0:T(8,128)} %get-tuple-element.4) | data formatting | bytes 1179648 | tf_op jit(solution)/shard_map/reshape | solution.py:982
  99.4 1.8 %reshape.15 = f32[6,6,2,1024]{3,2,1,0:T(2,128)} reshape(f32[72,1024]{1,0:T(8,128)} %get-tuple-element.5) | data formatting | bytes 589824 | tf_op jit(solution)/shard_map/reshape | solution.py:983

commit v4 on v3

--- a/solution.py
+++ b/solution.py
@@ -213,7 +213,7 @@
             act[chunk, :, cut] = jax.nn.gelu(values).astype(low_type)
             return carry
 
-        lax.fori_loop(0, act.shape[-1] // tile, hidden, 0)
+        lax.fori_loop(0, act.shape[-1] // tile, hidden, 0, unroll=True)
         start_y(1, chunk, act.at[chunk], w_out)
     for chunk in chunks:
         hold(chunk, act.at[chunk], w_out)
@@ -638,7 +638,7 @@
             ).astype(low_type)
             return carry
 
-        lax.fori_loop(0, HEADS // 2, head_pair, 0)
+        lax.fori_loop(0, HEADS // 2, head_pair, 0, unroll=True)
 
     for win in range(wins):
         attend(win)
@@ -870,7 +870,7 @@
         + attend_scratch
         + coarse_scratch(count, own_count, depth, merge_two, mlp_in, mlp_out, split_weight),
         compiler_params=pltpu.CompilerParams(
-            collective_id=3, has_side_effects=True, vmem_limit_bytes=62 * 1024 * 1024
+            collective_id=3, has_side_effects=True, vmem_limit_bytes=52 * 1024 * 1024
         ),
     )(
         tokens, qkv_weight, proj_weight, merge_one, merge_two, mlp_in, mlp_out, split_weight

time: 102 us -> 97.6 us (0.957)
  Pallas kernels: 94.8 us -> 90.3 us
    pallas_call x1, Pallas kernels: 94.8 us -> 90.3 us  [whole_block(): pl.pallas_call(functools.partial(whole_kernel, len(attend_scratch), rows...]
    unnamed x0 -> x4, local copies, waits for them, and re-layouts: none -> 1.89 us
    reshape x1, local copies, waits for them, and re-layouts: 2.22 us -> 1.16 us  [on_device(): fine_out = fine.reshape(rows, cols, levels, width).transpose(2, 0, 1, 3)]
where the time goes in v4:
time: 97.6 us; the launch traced here: 96 us
  Pallas kernels  90.3 us (93%)
  local copies, waits for them, and re-layouts  5.01 us (5%)
    pallas_call x1, Pallas kernels, whole_block(): pl.pallas_call(functools.partial(whole_kernel, len(attend_scratch), rows...  90.3 us

profile of v4, /device:TPU:0, one launch (start us, length us, event | category | flops | bytes accessed | tf_op | source)
XLA Modules:
  0.0 96.0 jit_solution(15823991620378989954)
XLA Ops:
  0.6 1.1 %reshape.13.refs_0_ = bf16[12,24,512]{2,1,0:T(8,128)(2,1)S(1)} reshape(bf16[12,12,2,512]{3,2,1,0:T(2,128)(2,1)} %bitcast.4) | data formatting | bytes 589824 | tf_op jit(solution)/shard_map/reshape | solution.py:978
  1.7 0.0 copy-start
  1.7 1.0 %copy-done = bf16[512,384]{1,0:T(8,128)(2,1)S(1)} copy-done((bf16[512,384]{1,0:T(8,128)(2,1)S(1)}, bf16[512,384]{1,0:T(8,128)(2,1)}, u32[]{:S(2)}) %copy-start) | copy-done | bytes 393240
  2.7 0.0 copy-start.1
  2.7 0.9 copy-done.1
  3.6 90.3 %shard_map.95 = (f32[12,24,512]{2,1,0:T(8,128)S(1)}, f32[72,1024]{1,0:T(8,128)S(1)}) custom-call(bf16[12,24,512]{2,1,0:T(8,128)(2,1)S(1)} %reshape.13.refs_0_, bf16[512,384]{1,0:T(8,128)(2,1)S(1)} %copy-done, bf16[512,128]{1,0:T(8,128)(2,1)S(1)} %copy-done.1, bf16[2048,256]{1,0:T(8,128)(2,1)} %refs_3_.1, bf16[512,2048]{1,0:T(8,128)(2,1)} %refs_4_.1, ...), custom_call_target="tpu_custom_call" | custom-call | tf_op jit(solution)/shard_map/pallas_call | solution.py:856
  93.9 1.2 %reshape.14 = f32[12,12,2,512]{3,2,1,0:T(2,128)} reshape(f32[12,24,512]{2,1,0:T(8,128)S(1)} %get-tuple-element.4) | data formatting | bytes 1179648 | tf_op jit(solution)/shard_map/reshape | solution.py:982
  95.1 0.9 reshape.15
Async XLA Ops:
  1.7 1.0 %copy-start = (bf16[512,384]{1,0:T(8,128)(2,1)S(1)}, bf16[512,384]{1,0:T(8,128)(2,1)}, u32[]{:S(2)}) copy-start(bf16[512,384]{1,0:T(8,128)(2,1)} %refs_1_.1) | copy-start | bytes 1179652
  2.7 0.9 copy-start.1
